TPU v7x, 32 devices: a whole 2x2x4 slice. The times are simulated.
32 devices in a mesh: replica: 16 (over z, x, core), shard: 2 (over y).
Axes of the slice: x: 2, y: 2, z: 4, core: 2. Of those that a mesh axis runs over, the one named last changes fastest.
Arguments:
- frames: bfloat16 [32768, 768], P(('replica', 'shard')), may hold values from -6 to 6
- cotangent: bfloat16 [32768, 768], P(('replica', 'shard')), may hold values from -6 to 6
- segment_ids: int32 [32, 1024], P(('replica', 'shard')), may hold values from 0 to 7, never falling along the last dimension, each value on 1 to 512 neighbouring positions
- norm_gain: bfloat16 [2, 768], P(None, 'shard'), may hold values from 0.099609375 to 1.8984375
- norm_bias: bfloat16 [2, 768], P(None, 'shard'), may hold values from -2 to 2
- w_qkv: bfloat16 [768, 2304], P('shard'), may hold values from -0.21875 to 0.21875
- qv_bias: bfloat16 [2, 768], P(None, 'shard'), may hold values from -2 to 2
- w_out: bfloat16 [768, 768], P('shard'), may hold values from -0.875 to 0.875
- out_bias: bfloat16 [2, 768], P(None, 'shard'), may hold values from -2 to 2
- w_up: bfloat16 [768, 3072], P(None, 'shard'), may hold values from -0.21875 to 0.21875
- up_bias: bfloat16 [3072], P('shard'), may hold values from -3 to 3
- w_down: bfloat16 [3072, 768], P('shard'), may hold values from -0.109375 to 0.109375
Outputs:
- out_frames: bfloat16 [32768, 768], P(('replica', 'shard'))
- d_frames: float32 [32768, 768], P(('replica', 'shard'))
- d_norm_gain: float32 [2, 768], P(None, 'shard')
- d_norm_bias: float32 [2, 768], P(None, 'shard')
- d_w_qkv: float32 [768, 2304], P('shard')
- d_qv_bias: float32 [2, 768], P(None, 'shard')
- d_w_out: float32 [768, 768], P('shard')
- d_out_bias: float32 [2, 768], P(None, 'shard')
- d_w_up: float32 [768, 3072], P(None, 'shard')
- d_up_bias: float32 [3072], P('shard')
- d_w_down: float32 [3072, 768], P('shard')
Inputs may be any that keep to these rules, and one draw needn't show every extreme that they name: `segment_ids`: each row numbers the documents of one sequence in order: never falling, every number of 0 to 7 used, no document longer than 512 frames, and one exactly that long in every row.
All inputs are finite; a program needn't handle non-finite values.
Results may differ from a plain program's by a relative error of at most 0.018.
Values may be sent and summed in bfloat16 or wider, within the bound.
No kernel may reach another device: no remote copies, remote signals or barrier semaphores. Data moves between devices by JAX's collectives and lax.ppermute only.
A program may use at most 256 MiB of HBM per device.

v0:
```python
import math

import jax
import jax.numpy as jnp
from jax import lax
from jax.sharding import PartitionSpec as P

H = 12


EPS = 1e-05
NEG = -1e30


def standardize(values):
    centered = values - jnp.mean(values, axis=1, keepdims=True)
    inverse = lax.rsqrt(jnp.mean(centered * centered, axis=1, keepdims=True) + EPS)
    return (centered * inverse, inverse)


def norm_back(grad_unit, unit, inverse):
    return inverse * (
        grad_unit
        - jnp.mean(grad_unit, axis=1, keepdims=True)
        - unit * jnp.mean(grad_unit * unit, axis=1, keepdims=True)
    )


def gelu_exact(values):
    return jax.nn.gelu(values, approximate=False)


def gelu_back(values, gradient):
    _, pull = jax.vjp(gelu_exact, values)
    return pull(gradient)[0]


def halves(array, which, axis):
    size = array.shape[axis] // 2
    return lax.slice_in_dim(array, which * size, (which + 1) * size, axis=axis)


def touching(query_seg, key_seg):
    return jnp.logical_and(query_seg[-1] >= key_seg[0], query_seg[0] <= key_seg[-1])


def keep_same(carry):
    return carry


def masked_scores(query_part, key_part, query_seg, key_seg):
    scale = 1.0 / math.sqrt(query_part.shape[2])
    raw = (
        jnp.einsum("qhd,khd->hqk", query_part, key_part, preferred_element_type=jnp.float32) * scale
    )
    same = query_seg[:, None] == key_seg[None, :]
    return jnp.where(same[None], raw, NEG)


def attend_forward(packed):
    queries, key_rows, value_rows, segment = packed
    outputs = []
    norms = []
    for query_pos in range(2):
        query_part = halves(queries, query_pos, 0)
        query_seg = halves(segment, query_pos, 0)
        span, heads, head_dim = query_part.shape
        peak = jnp.full((heads, span), NEG, jnp.float32)
        mass = jnp.zeros((heads, span), jnp.float32)
        for key_pos in range(2):
            key_part = halves(key_rows, key_pos, 0)
            key_seg = halves(segment, key_pos, 0)

            def grow(
                carry,
                key_part=key_part,
                key_seg=key_seg,
                query_part=query_part,
                query_seg=query_seg,
            ):
                old_peak, old_mass = carry
                scores = masked_scores(query_part, key_part, query_seg, key_seg)
                new_peak = jnp.maximum(old_peak, jnp.max(scores, axis=2))
                new_mass = old_mass * jnp.exp(old_peak - new_peak) + jnp.sum(
                    jnp.exp(scores - new_peak[:, :, None]), axis=2
                )
                return (new_peak, new_mass)

            peak, mass = lax.cond(touching(query_seg, key_seg), grow, keep_same, (peak, mass))
        log_norm = peak + jnp.log(mass)
        running = jnp.zeros((span, heads, head_dim), jnp.float32)
        for key_pos in range(2):
            key_part = halves(key_rows, key_pos, 0)
            value_part = halves(value_rows, key_pos, 0)
            key_seg = halves(segment, key_pos, 0)

            def spread(
                carry,
                key_part=key_part,
                value_part=value_part,
                key_seg=key_seg,
                query_part=query_part,
                query_seg=query_seg,
                log_norm=log_norm,
            ):
                scores = masked_scores(query_part, key_part, query_seg, key_seg)
                weights = jnp.exp(scores - log_norm[:, :, None]).astype(jnp.bfloat16)
                return carry + jnp.einsum(
                    "hqk,khd->qhd", weights, value_part, preferred_element_type=jnp.float32
                )

            running = lax.cond(touching(query_seg, key_seg), spread, keep_same, running)
        outputs.append(running)
        norms.append(log_norm)
    return (jnp.concatenate(outputs, axis=0), jnp.concatenate(norms, axis=1))


def attend_backward(packed):
    queries, key_rows, value_rows, segment, log_norm, grad_mixed, attended = packed
    scale = 1.0 / math.sqrt(queries.shape[2])
    row_dot = jnp.sum(grad_mixed * attended, axis=2).T
    query_grads = [jnp.zeros(halves(queries, 0, 0).shape, jnp.float32) for which in range(2)]
    key_grads = [jnp.zeros(halves(queries, 0, 0).shape, jnp.float32) for which in range(2)]
    value_grads = [jnp.zeros(halves(queries, 0, 0).shape, jnp.float32) for which in range(2)]
    for query_pos in range(2):
        query_part = halves(queries, query_pos, 0)
        query_seg = halves(segment, query_pos, 0)
        grad_part = halves(grad_mixed, query_pos, 0)
        norm_part = halves(log_norm, query_pos, 1)
        dot_part = halves(row_dot, query_pos, 1)
        for key_pos in range(2):
            key_part = halves(key_rows, key_pos, 0)
            value_part = halves(value_rows, key_pos, 0)
            key_seg = halves(segment, key_pos, 0)

            def accumulate(
                carry,
                query_part=query_part,
                query_seg=query_seg,
                grad_part=grad_part,
                norm_part=norm_part,
                dot_part=dot_part,
                key_part=key_part,
                value_part=value_part,
                key_seg=key_seg,
            ):
                part_query, part_key, part_value = carry
                scores = masked_scores(query_part, key_part, query_seg, key_seg)
                probs = jnp.exp(scores - norm_part[:, :, None])
                part_value = part_value + jnp.einsum(
                    "hqk,qhd->khd",
                    probs.astype(jnp.bfloat16),
                    grad_part,
                    preferred_element_type=jnp.float32,
                )
                grad_probs = jnp.einsum(
                    "qhd,khd->hqk", grad_part, value_part, preferred_element_type=jnp.float32
                )
                grad_scores = (probs * (grad_probs - dot_part[:, :, None])).astype(jnp.bfloat16)
                part_query = (
                    part_query
                    + jnp.einsum(
                        "hqk,khd->qhd", grad_scores, key_part, preferred_element_type=jnp.float32
                    )
                    * scale
                )
                part_key = (
                    part_key
                    + jnp.einsum(
                        "hqk,qhd->khd", grad_scores, query_part, preferred_element_type=jnp.float32
                    )
                    * scale
                )
                return (part_query, part_key, part_value)

            updated = lax.cond(
                touching(query_seg, key_seg),
                accumulate,
                keep_same,
                (query_grads[query_pos], key_grads[key_pos], value_grads[key_pos]),
            )
            query_grads[query_pos] = updated[0]
            key_grads[key_pos] = updated[1]
            value_grads[key_pos] = updated[2]
    return (
        jnp.concatenate(query_grads, axis=0),
        jnp.concatenate(key_grads, axis=0),
        jnp.concatenate(value_grads, axis=0),
    )


def local(
    frames,
    cotangent,
    segment_ids,
    norm_gain,
    norm_bias,
    w_qkv,
    qv_bias,
    w_out,
    out_bias,
    w_up,
    up_bias,
    w_down,
):
    rows, width = frames.shape
    seq_count, length = segment_ids.shape
    heads = H
    head_dim = width // heads
    shape_four = (seq_count, length, heads, head_dim)
    gathered = (
        lax.all_gather(norm_gain, "shard", axis=1, tiled=True),
        lax.all_gather(norm_bias, "shard", axis=1, tiled=True),
        lax.all_gather(w_qkv, "shard", axis=0, tiled=True),
        lax.all_gather(qv_bias, "shard", axis=1, tiled=True),
        lax.all_gather(w_out, "shard", axis=0, tiled=True),
        lax.all_gather(out_bias, "shard", axis=1, tiled=True),
    )
    gain_full = gathered[0].astype(jnp.float32)
    shift_full = gathered[1].astype(jnp.float32)
    qkv_full = gathered[2]
    qv_full = gathered[3].astype(jnp.float32)
    out_weight = gathered[4]
    outb_full = gathered[5].astype(jnp.float32)
    inputs = frames.astype(jnp.float32)
    unit_one, inverse_one = standardize(inputs)
    normed_one = (unit_one * gain_full[0] + shift_full[0]).astype(jnp.bfloat16)
    projected = jnp.dot(normed_one, qkv_full, preferred_element_type=jnp.float32)
    queries = (projected[:, :width] + qv_full[0]).astype(jnp.bfloat16).reshape(shape_four)
    key_rows = projected[:, width : 2 * width].astype(jnp.bfloat16).reshape(shape_four)
    value_rows = (projected[:, 2 * width :] + qv_full[1]).astype(jnp.bfloat16).reshape(shape_four)
    attended, log_norm = lax.map(attend_forward, (queries, key_rows, value_rows, segment_ids))
    mixed_low = attended.reshape(rows, width).astype(jnp.bfloat16)
    middle = (
        inputs + jnp.dot(mixed_low, out_weight, preferred_element_type=jnp.float32) + outb_full[0]
    )
    unit_two, inverse_two = standardize(middle)
    normed_two = (unit_two * gain_full[1] + shift_full[1]).astype(jnp.bfloat16)
    up_full, upb_full, down_full = (
        lax.all_gather(w_up, "shard", axis=1, tiled=True),
        lax.all_gather(up_bias, "shard", axis=0, tiled=True),
        lax.all_gather(w_down, "shard", axis=0, tiled=True),
    )
    hidden_pre = jnp.dot(normed_two, up_full, preferred_element_type=jnp.float32) + upb_full.astype(
        jnp.float32
    )
    activated = gelu_exact(hidden_pre).astype(jnp.bfloat16)
    branch_two = jnp.dot(activated, down_full, preferred_element_type=jnp.float32)
    result = middle + branch_two + outb_full[1]
    grad_out = cotangent.astype(jnp.float32)
    outb_grad_two = jnp.sum(grad_out, axis=0)
    up_back, down_back = (
        lax.all_gather(w_up, "shard", axis=1, tiled=True),
        lax.all_gather(w_down, "shard", axis=0, tiled=True),
    )
    grad_act = jnp.dot(cotangent, down_back.T, preferred_element_type=jnp.float32)
    grad_hidden = gelu_back(hidden_pre, grad_act).astype(jnp.bfloat16)
    down_grad = jnp.dot(activated.T, cotangent, preferred_element_type=jnp.float32)
    up_grad = jnp.dot(normed_two.T, grad_hidden, preferred_element_type=jnp.float32)
    upb_grad = jnp.sum(grad_hidden, axis=0, dtype=jnp.float32)
    grad_norm_two = jnp.dot(grad_hidden, up_back.T, preferred_element_type=jnp.float32)
    up_local, upb_local, down_local = (
        lax.psum_scatter(
            up_grad.astype(jnp.bfloat16), "shard", scatter_dimension=1, tiled=True
        ).astype(jnp.float32),
        lax.psum_scatter(
            upb_grad.astype(jnp.bfloat16), "shard", scatter_dimension=0, tiled=True
        ).astype(jnp.float32),
        lax.psum_scatter(
            down_grad.astype(jnp.bfloat16), "shard", scatter_dimension=0, tiled=True
        ).astype(jnp.float32),
    )
    up_summed, upb_summed, down_summed = (
        lax.psum(up_local.astype(jnp.bfloat16), "replica").astype(jnp.float32),
        lax.psum(upb_local.astype(jnp.bfloat16), "replica").astype(jnp.float32),
        lax.psum(down_local.astype(jnp.bfloat16), "replica").astype(jnp.float32),
    )
    gain_grad_two = jnp.sum(grad_norm_two * unit_two, axis=0)
    shift_grad_two = jnp.sum(grad_norm_two, axis=0)
    grad_middle = grad_out + norm_back(grad_norm_two * gain_full[1], unit_two, inverse_two)
    grad_branch = grad_middle.astype(jnp.bfloat16)
    outb_grad_one = jnp.sum(grad_branch, axis=0, dtype=jnp.float32)
    qkv_back, out_back = (
        lax.all_gather(w_qkv, "shard", axis=0, tiled=True),
        lax.all_gather(w_out, "shard", axis=0, tiled=True),
    )
    out_grad = jnp.dot(mixed_low.T, grad_branch, preferred_element_type=jnp.float32)
    grad_mixed = jnp.dot(grad_branch, out_back.T, preferred_element_type=jnp.float32).astype(
        jnp.bfloat16
    )
    grad_queries, grad_keys, grad_values = lax.map(
        attend_backward,
        (
            queries,
            key_rows,
            value_rows,
            segment_ids,
            log_norm,
            grad_mixed.reshape(shape_four),
            attended,
        ),
    )
    query_low = grad_queries.reshape(rows, width).astype(jnp.bfloat16)
    key_low = grad_keys.reshape(rows, width).astype(jnp.bfloat16)
    value_low = grad_values.reshape(rows, width).astype(jnp.bfloat16)
    grad_projected = jnp.concatenate([query_low, key_low, value_low], axis=1)
    qv_grad = jnp.stack(
        [
            jnp.sum(query_low, axis=0, dtype=jnp.float32),
            jnp.sum(value_low, axis=0, dtype=jnp.float32),
        ]
    )
    qkv_grad = jnp.dot(normed_one.T, grad_projected, preferred_element_type=jnp.float32)
    grad_norm_one = jnp.dot(grad_projected, qkv_back.T, preferred_element_type=jnp.float32)
    gain_grad_one = jnp.sum(grad_norm_one * unit_one, axis=0)
    shift_grad_one = jnp.sum(grad_norm_one, axis=0)
    grad_inputs = grad_middle + norm_back(grad_norm_one * gain_full[0], unit_one, inverse_one)
    gain_grads = jnp.stack([gain_grad_one, gain_grad_two])
    shift_grads = jnp.stack([shift_grad_one, shift_grad_two])
    outb_grads = jnp.stack([outb_grad_one, outb_grad_two])
    local_grads = (
        lax.psum_scatter(
            gain_grads.astype(jnp.bfloat16), "shard", scatter_dimension=1, tiled=True
        ).astype(jnp.float32),
        lax.psum_scatter(
            shift_grads.astype(jnp.bfloat16), "shard", scatter_dimension=1, tiled=True
        ).astype(jnp.float32),
        lax.psum_scatter(
            qkv_grad.astype(jnp.bfloat16), "shard", scatter_dimension=0, tiled=True
        ).astype(jnp.float32),
        lax.psum_scatter(
            qv_grad.astype(jnp.bfloat16), "shard", scatter_dimension=1, tiled=True
        ).astype(jnp.float32),
        lax.psum_scatter(
            out_grad.astype(jnp.bfloat16), "shard", scatter_dimension=0, tiled=True
        ).astype(jnp.float32),
        lax.psum_scatter(
            outb_grads.astype(jnp.bfloat16), "shard", scatter_dimension=1, tiled=True
        ).astype(jnp.float32),
    )
    summed = (
        lax.psum(local_grads[0].astype(jnp.bfloat16), "replica").astype(jnp.float32),
        lax.psum(local_grads[1].astype(jnp.bfloat16), "replica").astype(jnp.float32),
        lax.psum(local_grads[2].astype(jnp.bfloat16), "replica").astype(jnp.float32),
        lax.psum(local_grads[3].astype(jnp.bfloat16), "replica").astype(jnp.float32),
        lax.psum(local_grads[4].astype(jnp.bfloat16), "replica").astype(jnp.float32),
        lax.psum(local_grads[5].astype(jnp.bfloat16), "replica").astype(jnp.float32),
    )
    return (
        result.astype(jnp.bfloat16),
        grad_inputs,
        summed[0],
        summed[1],
        summed[2],
        summed[3],
        summed[4],
        summed[5],
        up_summed,
        upb_summed,
        down_summed,
    )


def solution(mesh):
    placed = (
        P(("replica", "shard"), None),
        P(("replica", "shard"), None),
        P(("replica", "shard"), None),
        P(None, "shard"),
        P(None, "shard"),
        P("shard", None),
        P(None, "shard"),
        P("shard", None),
        P(None, "shard"),
        P(None, "shard"),
        P("shard"),
        P("shard", None),
    )
    return jax.shard_map(
        local,
        mesh=mesh,
        in_specs=placed,
        out_specs=(
            P(("replica", "shard"), None),
            P(("replica", "shard"), None),
            P(None, "shard"),
            P(None, "shard"),
            P("shard", None),
            P(None, "shard"),
            P("shard", None),
            P(None, "shard"),
            P(None, "shard"),
            P("shard"),
            P("shard", None),
        ),
        check_vma=False,
    )
```

profile of v0, /device:TPU:0, one launch (start us, length us, event | category | flops | bytes accessed | tf_op | source)
XLA Modules:
  0.0 748.9 jit_solution(15768583942616573431)
XLA Ops:
  23.7 5.3 all_gather.31
  29.0 4.3 all_gather.32
  33.5 4.3 all_gather.34
  37.9 4.3 all_gather.36
  42.8 4.5 all-gather
  48.9 13.0 %all-gather.6.cloned.1.call-done = bf16[768,2304]{1,0:T(8,128)(2,1)} async-done(((bf16[384,2304]{1,0:T(8,128)(2,1)}), bf16[768,2304]{1,0:T(8,128)(2,1)}) %all-gather.6.cloned.1.call-update) | async-done | bytes 3538960 | tf_op jit(solution)/shard_map/all_gather | solution.py:214
  61.9 7.9 %fusion.108 = (bf16[1024,2304]{1,0:T(8,128)(2,1)}, f32[1024,2304]{1,0:T(8,128)S(1)}) fusion(bf16[768,2304]{1,0:T(8,128)(2,1)} %all-gather.6.cloned.1.call-done, bf16[1024,768]{0,1:T(8,128)(2,1)S(1)} %copy.79, f32[768]{0:T(1024)S(1)} %get-tuple-element.583, f32[768]{0:T(1024)S(1)} %get-tuple-element.581, f32[1024]{0:T(1024)S(1)} %add_rsqrt_fusion.1, ...), kind=kOutput, calls=%fused_computation.198 | convolution fusion | flops 3630956544 | bytes 19281920 | tf_op jit(solution)/shard_map/dot_general | solution.py:228
  82.3 7.4 conditional.12
  82.6 3.2 fusion
  86.4 3.3 exponential_reduce_fusion
  89.7 7.3 conditional.13
  97.8 8.4 %conditional.14 = (f32[512,12,64]{0,2,1:T(8,128)}) conditional(s32[]{:T(128)} %bitcast.14, () %tuple.120, (s32[512]{0:T(512)S(1)}, bf16[512,12,64]{0,2,1:T(8,128)(2,1)S(1)}, bf16[512,12,64]{0,2,1:T(8,128)(2,1)}, f32[12,512]{1,0:T(8,128)S(1)}, bf16[512,12,64]{0,2,1:T(8,128)(2,1)}) %tuple.314), branch_computations={%region_10.11_spmd, %region_11.12_spmd} | conditional | flops 818151424 | bytes 4483080 | solution.py:112
  98.1 8.1 %fusion.6 = f32[512,12,64]{0,2,1:T(8,128)} fusion(bf16[512,12,64]{0,2,1:T(8,128)(2,1)} %get-tuple-element.287, f32[12,512]{1,0:T(8,128)S(1)} %get-tuple-element.286, pred[512,512]{1,0:T(8,128)(4,1)S(1)} %broadcast_compare_fusion.2, bf16[512,12,64]{0,2,1:T(8,128)(2,1)S(1)} %get-tuple-element.284, bf16[512,12,64]{0,2,1:T(8,128)(2,1)} %get-tuple-element.285), kind=kOutput, calls=%fused_computation.15 | convolution fusion | flops 817889280 | bytes 4218880 | tf_op jit(solution)/shard_map/while/body/eval_jaxpr/cond/branch_1_fun/hqk,khd->qhd/dot_general | solution.py:108
  106.2 8.9 %conditional.15 = (f32[512,12,64]{0,2,1:T(8,128)}) conditional(s32[]{:T(128)} %bitcast.13, f32[512,12,64]{0,2,1:T(8,128)} %get-tuple-element.687, (s32[512]{0:T(512)S(1)}, s32[512]{0:T(512)S(1)}, bf16[512,12,64]{0,2,1:T(8,128)(2,1)S(1)}, bf16[512,12,64]{0,2,1:T(8,128)(2,1)S(1)}, f32[12,512]{1,0:T(8,128)S(1)}, ...), branch_computations={%region_12.13_spmd, %region_13.14_spmd} | conditional | flops 818544640 | bytes 6057992 | solution.py:112
  106.8 8.3 %bitcast_add_fusion = f32[512,12,64]{0,2,1:T(8,128)} fusion(f32[512,12,64]{0,2,1:T(8,128)} %get-tuple-element.288, bf16[512,12,64]{0,2,1:T(8,128)(2,1)} %get-tuple-element.294, f32[12,512]{1,0:T(8,128)S(1)} %get-tuple-element.293, pred[512,512]{1,0:T(8,128)(4,1)S(1)} %broadcast_compare_fusion.3, bf16[512,12,64]{0,2,1:T(8,128)(2,1)S(1)} %get-tuple-element.291, ...), kind=kOutput, calls=%fused_computation.23 | convolution fusion | flops 818282496 | bytes 5791744 | tf_op jit(solution)/shard_map/while/body/eval_jaxpr/cond/branch_1_fun/hqk,khd->qhd/dot_general | solution.py:108
  117.4 7.6 %conditional.16 = (f32[12,512]{1,0:T(8,128)}, f32[12,512]{1,0:T(8,128)S(1)}) conditional(s32[]{:T(128)} %bitcast.23, () %tuple.127, (s32[512]{0:T(512)S(1)}, s32[512]{0:T(512)S(1)}, bf16[512,12,64]{0,2,1:T(8,128)(2,1)}, bf16[512,12,64]{0,2,1:T(8,128)(2,1)}) %tuple.316), branch_computations={%region_14.15_spmd, %region_15.0_spmd} | conditional | flops 424953856 | bytes 27725840 | solution.py:89
  117.6 3.4 fusion.15
  121.7 3.3 exponential_reduce_fusion.2
  125.1 8.4 %conditional.17 = ((f32[12,512]{1,0:T(8,128)}, f32[12,512]{1,0:T(8,128)S(1)})) conditional(s32[]{:T(128)} %bitcast.22, (f32[12,512]{1,0:T(8,128)}, f32[12,512]{1,0:T(8,128)S(1)}) %conditional.16, (s32[512]{0:T(512)S(1)}, bf16[512,12,64]{0,2,1:T(8,128)(2,1)}, bf16[512,12,64]{0,2,1:T(8,128)(2,1)S(1)}, f32[12,512]{1,0:T(8,128)}, ...), branch_computations={%region_18.19_spmd, %region_19.0_spmd} | conditional | flops 424947712 | bytes 27846680 | solution.py:89
  125.5 3.2 fusion.16
  134.2 8.3 %conditional.18 = (f32[512,12,64]{0,2,1:T(8,128)}) conditional(s32[]{:T(128)} %bitcast.23, () %tuple.126, (s32[512]{0:T(512)S(1)}, s32[512]{0:T(512)S(1)}, bf16[512,12,64]{0,2,1:T(8,128)(2,1)}, bf16[512,12,64]{0,2,1:T(8,128)(2,1)S(1)}, f32[12,512]{1,0:T(8,128)S(1)}, /*index=5*/bf16[512,12,64]{0,2,1:T(8,128)(2,1)}) %tuple.317), branch_computations={%region_22.23_spmd, %region_23.24_spmd} | conditional | flops 818151424 | bytes 4485128 | solution.py:112
  134.5 8.0 %fusion.21 = f32[512,12,64]{0,2,1:T(8,128)} fusion(bf16[512,12,64]{0,2,1:T(8,128)(2,1)} %get-tuple-element.309, f32[12,512]{1,0:T(8,128)S(1)} %get-tuple-element.308, pred[512,512]{1,0:T(8,128)(4,1)S(1)} %broadcast_compare_fusion.6, bf16[512,12,64]{0,2,1:T(8,128)(2,1)} %get-tuple-element.306, bf16[512,12,64]{0,2,1:T(8,128)(2,1)S(1)} %get-tuple-element.307), kind=kOutput, calls=%fused_computation.42 | convolution fusion | flops 817889280 | bytes 4218880 | tf_op jit(solution)/shard_map/while/body/eval_jaxpr/cond/branch_1_fun/hqk,khd->qhd/dot_general | solution.py:108
  142.5 9.0 %conditional.19 = (f32[512,12,64]{0,2,1:T(8,128)}) conditional(s32[]{:T(128)} %bitcast.22, f32[512,12,64]{0,2,1:T(8,128)} %get-tuple-element.690, (s32[512]{0:T(512)S(1)}, bf16[512,12,64]{0,2,1:T(8,128)(2,1)}, bf16[512,12,64]{0,2,1:T(8,128)(2,1)S(1)}, f32[12,512]{1,0:T(8,128)S(1)}, bf16[512,12,64]{0,2,1:T(8,128)(2,1)}, ...), branch_computations={%region_24.25_spmd, %region_25.26_spmd} | conditional | flops 818544640 | bytes 6055944 | solution.py:112
  142.9 8.6 %bitcast_add_fusion.1 = f32[512,12,64]{0,2,1:T(8,128)} fusion(f32[512,12,64]{0,2,1:T(8,128)} %get-tuple-element.310, bf16[512,12,64]{0,2,1:T(8,128)(2,1)} %get-tuple-element.315, f32[12,512]{1,0:T(8,128)S(1)} %get-tuple-element.314, pred[512,512]{1,0:T(8,128)(4,1)S(1)} %broadcast_compare_fusion.7, bf16[512,12,64]{0,2,1:T(8,128)(2,1)} %get-tuple-element.312, ...), kind=kOutput, calls=%fused_computation.50 | convolution fusion | flops 818282496 | bytes 5791744 | tf_op jit(solution)/shard_map/while/body/eval_jaxpr/cond/branch_1_fun/hqk,khd->qhd/dot_general | solution.py:108
  153.7 3.4 fusion.109
  159.3 39.0 %multiply_convert_fusion.4 = (bf16[1024,3072]{1,0:T(8,128)(2,1)}, f32[1024,3072]{1,0:T(8,128)}, f32[1024,3072]{1,0:T(8,128)}) fusion(f32[3072]{0:T(1024)S(1)} %bitcast.201, bf16[768,3072]{1,0:T(8,128)(2,1)} %all-gather.10.cloned.1.call-done, f32[1024,768]{0,1:T(8,128)} %copy-done.8, f32[768]{0:T(1024)S(1)} %get-tuple-element.582, ...), kind=kOutput, calls=%fused_computation.101 | convolution fusion | flops 5043388416 | bytes 39348224 | tf_op jit(solution)/shard_map/dot_general | solution.py:244
  198.3 16.4 %all-gather.12.cloned.1.call-done = bf16[3072,768]{1,0:T(8,128)(2,1)} async-done(((bf16[1536,768]{1,0:T(8,128)(2,1)}), bf16[3072,768]{1,0:T(8,128)(2,1)}) %all-gather.12.cloned.1.call-update) | async-done | bytes 4718608 | tf_op jit(solution)/shard_map/all_gather | solution.py:242
  214.6 17.3 %fusion.112 = (bf16[3072]{0:T(1024)(128)(2,1)}, bf16[1024,3072]{1,0:T(8,128)(2,1)}) fusion(f32[1024,3072]{1,0:T(8,128)} %get-tuple-element.602, bf16[1024,768]{1,0:T(8,128)(2,1)S(1)} %copy-done.23, bf16[3072,768]{1,0:T(8,128)(2,1)} %all-gather.12.cloned.1.call-done, f32[1024,3072]{1,0:T(8,128)} %get-tuple-element.633, f32[3072]{0:T(1024)S(1)} %bitcast.202), kind=kOutput, calls=%fused_computation.202 | convolution fusion | flops 4882166784 | bytes 37767168 | tf_op jit(solution)/shard_map/dot_general | solution.py:256
  232.0 10.5 %fusion.110 = (bf16[768]{0:T(1024)(128)(2,1)}, f32[1024,768]{1,0:T(8,128)}) fusion(bf16[1024,3072]{1,0:T(8,128)(2,1)} %get-tuple-element.639, bf16[768,3072]{1,0:T(8,128)(2,1)} %all-gather.10.cloned.1.call-done), kind=kOutput, calls=%fused_computation.200 | convolution fusion | flops 4832623616 | bytes 14157312 | tf_op jit(solution)/shard_map/dot_general | solution.py:261
  242.5 3.7 copy.88
  246.2 3.6 multiply_reduce_fusion
  255.4 3.4 convolution_convert_fusion.3
  260.8 14.6 %conditional.20 = (f32[512,12,64]{0,2,1:T(8,128)}, f32[512,12,64]{0,2,1:T(8,128)S(1)}, f32[512,12,64]{0,2,1:T(8,128)S(1)}) conditional(s32[]{:T(128)} %bitcast.14, () %tuple.132, (s32[512]{0:T(512)S(1)}, bf16[512,12,64]{0,2,1:T(8,128)(2,1)S(1)}, bf16[512,12,64]{0,2,1:T(8,128)(2,1)S(1)}, f32[12,512]{1,0:T(8,128)S(1)}, ...), branch_computations={%region_31.32_spmd.clone, %region_32.33_spmd.clone} | conditional | flops 2045771776 | bytes 77146216 | solution.py:176
  262.9 4.8 multiply_convert_fusion.3
  272.0 3.1 fusion.59
  277.1 16.9 %conditional.21 = (f32[512,12,64]{0,2,1:T(8,128)}, f32[512,12,64]{0,2,1:T(8,128)S(1)}, f32[512,12,64]{0,2,1:T(8,128)}) conditional(s32[]{:T(128)} %bitcast.13, f32[512,12,64]{0,2,1:T(8,128)} %get-tuple-element.394, (s32[512]{0:T(512)S(1)}, s32[512]{0:T(512)S(1)}, bf16[512,12,64]{0,2,1:T(8,128)(2,1)S(1)}, bf16[512,12,64]{0,2,1:T(8,128)(2,1)S(1)}, ...), branch_computations={%region_33.34_spmd, %region_34.35_spmd} | conditional | flops 2046164992 | bytes 75575376 | solution.py:176
  279.1 4.8 multiply_convert_fusion
  284.0 4.6 bitcast_add_fusion.2
  289.7 4.3 fusion.34
  295.2 18.5 %conditional.22 = (f32[512,12,64]{0,2,1:T(8,128)}, f32[512,12,64]{0,2,1:T(8,128)}, f32[512,12,64]{0,2,1:T(8,128)}) conditional(s32[]{:T(128)} %bitcast.23, (f32[512,12,64]{0,2,1:T(8,128)}, f32[512,12,64]{0,2,1:T(8,128)}) %tuple.289, (s32[512]{0:T(512)S(1)}, s32[512]{0:T(512)S(1)}, bf16[512,12,64]{0,2,1:T(8,128)(2,1)}, ...), branch_computations={%region_35.36_spmd, %region_36.37_spmd} | conditional | flops 2046558208 | bytes 105459936 | solution.py:176
  298.9 4.8 multiply_convert_fusion.1
  306.0 3.1 multiply_bitcast_fusion.1
  309.2 3.3 bitcast_add_fusion.3
  313.7 21.3 %conditional.23 = (f32[512,12,64]{0,2,1:T(8,128)}, f32[512,12,64]{0,2,1:T(8,128)}, f32[512,12,64]{0,2,1:T(8,128)}) conditional(s32[]{:T(128)} %bitcast.22, (f32[512,12,64]{0,2,1:T(8,128)}, f32[512,12,64]{0,2,1:T(8,128)}, f32[512,12,64]{0,2,1:T(8,128)}) %tuple.287, (s32[512]{0:T(512)S(1)}, bf16[512,12,64]{0,2,1:T(8,128)(2,1)}, ...), branch_computations={%region_37.38_spmd, %region_38.39_spmd} | conditional | flops 2046951424 | bytes 91302032 | solution.py:176
  317.2 4.8 multiply_convert_fusion.2
  324.3 5.1 bitcast_add_fusion.7
  329.5 5.5 bitcast_add_fusion.6
  343.2 5.9 convolution_convert_fusion.2
  349.2 9.7 %convolution_convert_fusion.1 = bf16[768,3072]{1,0:T(8,128)(2,1)} fusion(bf16[1024,3072]{1,0:T(8,128)(2,1)} %get-tuple-element.639, f32[1024,768]{0,1:T(8,128)} %copy-done.8, f32[768]{0:T(1024)S(1)} %copy-done.68, f32[768]{0:T(1024)S(1)} %get-tuple-element.580, f32[1024]{0:T(1024)S(1)} %add_rsqrt_fusion, f32[1024]{0:T(1024)S(1)} %broadcast_multiply_fusion.4), kind=kOutput, calls=%fused_computation.116 | convolution fusion | flops 4838129664 | bytes 14170112 | tf_op jit(solution)/shard_map/dot_general | solution.py:259
  360.3 9.6 %convolution_convert_fusion = bf16[3072,768]{1,0:T(8,128)(2,1)} fusion(bf16[1024,3072]{1,0:T(8,128)(2,1)} %get-tuple-element.601, bf16[1024,768]{1,0:T(8,128)(2,1)S(1)} %copy-done.24), kind=kOutput, calls=%fused_computation.115 | convolution fusion | flops 4834197504 | bytes 12582912 | tf_op jit(solution)/shard_map/dot_general | solution.py:258
  371.4 9.0 %fusion.111 = (bf16[768]{0:T(1024)(128)(2,1)S(1)}, f32[1024,768]{1,0:T(8,128)}) fusion(bf16[768,2304]{1,0:T(8,128)(2,1)} %all-gather.6.cloned.1.call-done, bf16[1024,768]{0,1:T(8,128)(2,1)} %bitcast.159, bf16[1024,768]{0,1:T(8,128)(2,1)} %bitcast.155, bf16[1024,768]{0,1:T(8,128)(2,1)} %bitcast.157), kind=kOutput, calls=%fused_computation.201 | convolution fusion | flops 3638820096 | bytes 11404800 | tf_op jit(solution)/shard_map/dot_general | solution.py:314
  380.4 3.5 copy.89
  390.1 6.9 reduce-scatter.17.cloned.1.call-done
  397.0 62.9 %reduce-scatter.21.cloned.1.call-done = bf16[768,1536]{1,0:T(8,128)(2,1)} async-done(((bf16[768,3072]{1,0:T(8,128)(2,1)}), bf16[768,1536]{1,0:T(8,128)(2,1)}) %reduce-scatter.21.cloned.1.call-update) | async-done | bytes 2359312 | tf_op jit(solution)/shard_map/reduce_scatter | solution.py:263
  459.8 63.0 %reduce-scatter.23.cloned.1.call-done = bf16[1536,768]{1,0:T(8,128)(2,1)} async-done(((bf16[3072,768]{1,0:T(8,128)(2,1)}), bf16[1536,768]{1,0:T(8,128)(2,1)}) %reduce-scatter.23.cloned.1.call-update) | async-done | bytes 2359312 | tf_op jit(solution)/shard_map/reduce_scatter | solution.py:269
  524.2 5.5 fusion.81
  529.7 3.7 copy.93
  533.4 9.5 %add_convert_fusion.1 = bf16[1024,768]{0,1:T(8,128)(2,1)} fusion(f32[1024,768]{0,1:T(8,128)S(1)} %copy-done.10, bf16[1024,3072]{1,0:T(8,128)(2,1)} %get-tuple-element.601, bf16[3072,768]{1,0:T(8,128)(2,1)} %all-gather.12.cloned.1.call-done, f32[768]{0:T(1024)S(1)} %copy-done.66), kind=kOutput, calls=%fused_computation.149 | convolution fusion | flops 4834197504 | bytes 15731712 | tf_op jit(solution)/shard_map/dot_general | solution.py:248
  545.5 5.0 all-reduce
  552.5 9.8 %reduce-scatter.25.cloned.1.call-done = bf16[384,2]{1,0:T(8,128)(2,1)} async-done(((bf16[768,2]{1,0:T(8,128)(2,1)}), bf16[384,2]{1,0:T(8,128)(2,1)}) %reduce-scatter.25.cloned.1.call-update) | async-done | bytes 1552
  563.3 12.1 %reduce-scatter.31.cloned.1.call-done = bf16[384,2]{1,0:T(8,128)(2,1)} async-done(((bf16[768,2]{1,0:T(8,128)(2,1)}), bf16[384,2]{1,0:T(8,128)(2,1)}) %reduce-scatter.31.cloned.1.call-update) | async-done | bytes 1552
  576.4 64.0 %all-reduce.1 = (bf16[2,384]{1,0:T(2,128)(2,1)S(1)}, bf16[2,384]{1,0:T(2,128)(2,1)S(1)}, bf16[2,384]{1,0:T(2,128)(2,1)S(1)}, bf16[2,384]{1,0:T(2,128)(2,1)S(1)}, bf16[1536]{0:T(1024)(128)(2,1)S(1)}) all-reduce(bf16[2,384]{1,0:T(2,128)(2,1)S(1)} %copy.96, ...), channel_id=1, replica_groups=mesh['replica'=16,'shard'=2] {'replica'}, use_global_device_ids=true, to_apply=%region_44.45 | all-reduce | flops 4608 | bytes 18432 | tf_op jit(solution)/shard_map/psum | solution.py:342
  643.4 88.3 %all-reduce.5.cloned.1.call-done = (bf16[384,2304]{1,0:T(8,128)(2,1)}, bf16[384,768]{1,0:T(8,128)(2,1)}, bf16[768,1536]{1,0:T(8,128)(2,1)}, bf16[1536,768]{1,0:T(8,128)(2,1)}) async-done(((bf16[384,2304]{1,0:T(8,128)(2,1)}, bf16[384,768]{1,0:T(8,128)(2,1)}, bf16[768,1536]{1,0:T(8,128)(2,1)}, bf16[1536,768]{1,0:T(8,128)(2,1)}), (bf16[384,2304]{1,0:T(8,128)(2,1)}, bf16[384,768]{1,0:T(8,128)(2,1)}, ...) | async-done | bytes 7077904 | tf_op jit(solution)/shard_map/psum | solution.py:344
  731.6 4.6 convert_element_type.275
  (303 shorter events, 108.3 us)
Async XLA Ops:
  7.2 54.7 %all-gather.6.cloned.1.call-start = ((), (), s32[]{:S(2)}) async-start(), calls=%async_computation.8 | async-start | bytes 5308416 | tf_op jit(solution)/shard_map/all_gather | solution.py:214
  7.9 145.7 %all-gather.8.cloned.1.call-start = ((), (), s32[]{:S(2)}) async-start(), calls=%async_computation.9 | async-start | bytes 1769472 | tf_op jit(solution)/shard_map/all_gather | solution.py:216
  8.7 150.6 %all-gather.10.cloned.1.call-start = ((), (), s32[]{:S(2)}) async-start(), calls=%async_computation.10 | async-start | bytes 7077888 | tf_op jit(solution)/shard_map/all_gather | solution.py:240
  9.4 14.3 %copy-start.73 = (bf16[2,384]{1,0:T(2,128)(2,1)S(1)}, bf16[2,384]{1,0:T(2,128)(2,1)}, u32[]{:S(2)}) copy-start(bf16[2,384]{1,0:T(2,128)(2,1)} %param.39) | copy-start | bytes 4612
  9.4 19.6 %copy-start.74 = (bf16[2,384]{1,0:T(2,128)(2,1)S(1)}, bf16[2,384]{1,0:T(2,128)(2,1)}, u32[]{:S(2)}) copy-start(bf16[2,384]{1,0:T(2,128)(2,1)} %param.40) | copy-start | bytes 4612
  9.4 24.0 %copy-start.75 = (bf16[2,384]{1,0:T(2,128)(2,1)S(1)}, bf16[2,384]{1,0:T(2,128)(2,1)}, u32[]{:S(2)}) copy-start(bf16[2,384]{1,0:T(2,128)(2,1)} %param.42) | copy-start | bytes 4612
  9.4 28.4 %copy-start.76 = (bf16[2,384]{1,0:T(2,128)(2,1)S(1)}, bf16[2,384]{1,0:T(2,128)(2,1)}, u32[]{:S(2)}) copy-start(bf16[2,384]{1,0:T(2,128)(2,1)} %param.44) | copy-start | bytes 4612
  9.4 33.4 %copy-start.71 = (bf16[1536]{0:T(1024)(128)(2,1)S(1)}, bf16[1536]{0:T(1024)(128)(2,1)}, u32[]{:S(2)}) copy-start(bf16[1536]{0:T(1024)(128)(2,1)} %param.46) | copy-start | bytes 9220
  9.5 37.9 %copy-start.22 = (bf16[1024,768]{1,0:T(8,128)(2,1)S(1)}, bf16[1024,768]{1,0:T(8,128)(2,1)}, u32[]{:S(2)}) copy-start(bf16[1024,768]{1,0:T(8,128)(2,1)} %param.37) | copy-start | bytes 4718596
  9.5 205.2 %all-gather.12.cloned.1.call-start = ((), (), s32[]{:S(2)}) async-start(), calls=%async_computation.11 | async-start | bytes 7077888 | tf_op jit(solution)/shard_map/all_gather | solution.py:242
  10.0 380.0 %reduce-scatter.19.cloned.1.call-start = ((), (), s32[]{:S(2)}) async-start(), calls=%async_computation.13 | async-start | bytes 1769472 | tf_op jit(solution)/shard_map/reduce_scatter | solution.py:334
  10.1 124.1 %copy-start.51 = (s32[1,512]{1,0:T(1,128)}, s32[1,512]{1,0:T(1,128)S(1)}, u32[]{:S(2)}) copy-start(s32[1,512]{1,0:T(1,128)S(1)} %get-tuple-element.623) | copy-start | bytes 6148
  10.1 132.4 %copy-start.49 = (s32[1,512]{1,0:T(1,128)}, s32[1,512]{1,0:T(1,128)S(1)}, u32[]{:S(2)}) copy-start(s32[1,512]{1,0:T(1,128)S(1)} %get-tuple-element.624) | copy-start | bytes 6148
  22.9 130.8 %copy-start.2 = (bf16[1024,768]{0,1:T(8,128)(2,1)}, bf16[1024,768]{0,1:T(8,128)(2,1)S(1)}, u32[]{:S(2)}) copy-start(bf16[1024,768]{0,1:T(8,128)(2,1)S(1)} %copy.79) | copy-start | bytes 4718596
  23.2 46.6 %copy-start.53 = (f32[1024]{0:T(1024)}, f32[1024]{0:T(1024)S(1)}, u32[]{:S(2)}) copy-start(f32[1024]{0:T(1024)S(1)} %broadcast_multiply_fusion.5) | copy-start | bytes 12292
  23.7 46.2 %copy-start.57 = (f32[1024]{0:T(1024)}, f32[1024]{0:T(1024)S(1)}, u32[]{:S(2)}) copy-start(f32[1024]{0:T(1024)S(1)} %add_rsqrt_fusion.1) | copy-start | bytes 12292
  29.0 40.8 %copy-start.55 = (f32[768]{0:T(1024)}, f32[768]{0:T(1024)S(1)}, u32[]{:S(2)}) copy-start(f32[768]{0:T(1024)S(1)} %get-tuple-element.581) | copy-start | bytes 9220
  33.4 36.4 %copy-start.69 = (f32[768]{0:T(1024)}, f32[768]{0:T(1024)S(1)}, u32[]{:S(2)}) copy-start(f32[768]{0:T(1024)S(1)} %get-tuple-element.583) | copy-start | bytes 9220
  33.4 125.8 %copy-start.67 = (f32[768]{0:T(1024)}, f32[768]{0:T(1024)S(1)}, u32[]{:S(2)}) copy-start(f32[768]{0:T(1024)S(1)} %get-tuple-element.582) | copy-start | bytes 9220
  72.2 34.0 %copy-start = (bf16[512,768]{0,1:T(8,128)(2,1)}, bf16[512,768]{0,1:T(8,128)(2,1)S(1)}, u32[]{:S(2)}) copy-start(bf16[512,768]{0,1:T(8,128)(2,1)S(1)} %copy.80) | copy-start | bytes 2359300
  77.4 65.1 %copy-start.4 = (bf16[512,768]{0,1:T(8,128)(2,1)}, bf16[512,768]{0,1:T(8,128)(2,1)S(1)}, u32[]{:S(2)}) copy-start(bf16[512,768]{0,1:T(8,128)(2,1)S(1)} %copy.82) | copy-start | bytes 2359300
  97.8 8.4 %copy-start.59 = (f32[12,512]{1,0:T(8,128)}, f32[12,512]{1,0:T(8,128)S(1)}, u32[]{:S(2)}) copy-start(f32[12,512]{1,0:T(8,128)S(1)} %log_add_fusion.1) | copy-start | bytes 73732
  125.0 9.1 %copy-start.6 = (bf16[512,768]{0,1:T(8,128)(2,1)S(1)}, bf16[512,768]{0,1:T(8,128)(2,1)}, u32[]{:S(2)}) copy-start(bf16[512,768]{0,1:T(8,128)(2,1)} %copy.81) | copy-start | bytes 2359300
  134.2 8.3 %copy-start.61 = (f32[12,512]{1,0:T(8,128)}, f32[12,512]{1,0:T(8,128)S(1)}, u32[]{:S(2)}) copy-start(f32[12,512]{1,0:T(8,128)S(1)} %log_add_fusion) | copy-start | bytes 73732
  153.6 3.5 copy-start.35
  159.3 55.3 %copy-start.23 = (bf16[1024,768]{1,0:T(8,128)(2,1)S(1)}, bf16[1024,768]{1,0:T(8,128)(2,1)}, u32[]{:S(2)}) copy-start(bf16[1024,768]{1,0:T(8,128)(2,1)} %param.37) | copy-start | bytes 4718596
  242.5 3.7 copy-start.9
  246.1 3.6 copy-start.11
  246.2 3.6 copy-start.29
  251.2 4.2 copy-start.77
  255.3 141.6 %reduce-scatter.17.cloned.1.call-start = ((), (), s32[]{:S(2)}) async-start(), calls=%async_computation.12 | async-start | bytes 5308416 | tf_op jit(solution)/shard_map/reduce_scatter | solution.py:328
  255.4 3.5 copy-start.19
  255.4 3.5 copy-start.20
  260.8 14.7 %copy-start.5 = (bf16[512,768]{0,1:T(8,128)(2,1)S(1)}, bf16[512,768]{0,1:T(8,128)(2,1)}, u32[]{:S(2)}) copy-start(bf16[512,768]{0,1:T(8,128)(2,1)} %copy-done.4) | copy-start | bytes 2359300
  260.8 14.7 %copy-start.37 = (bf16[512,768]{0,1:T(8,128)(2,1)S(1)}, bf16[512,768]{0,1:T(8,128)(2,1)}, u32[]{:S(2)}) copy-start(bf16[512,768]{0,1:T(8,128)(2,1)} %copy.84) | copy-start | bytes 2359300
  260.8 14.7 %copy-start.50 = (s32[1,512]{1,0:T(1,128)S(1)}, s32[1,512]{1,0:T(1,128)}, u32[]{:S(2)}) copy-start(s32[1,512]{1,0:T(1,128)} %copy-done.49) | copy-start | bytes 6148
  275.5 18.5 %copy-start.62 = (f32[12,512]{1,0:T(8,128)S(1)}, f32[12,512]{1,0:T(8,128)}, u32[]{:S(2)}) copy-start(f32[12,512]{1,0:T(8,128)} %copy-done.61) | copy-start | bytes 73732
  298.9 4.8 copy-start.13
  306.0 6.5 copy-start.14
  313.7 22.8 %copy-start.15 = (f32[512,12,64]{0,2,1:T(8,128)S(1)}, f32[512,12,64]{0,2,1:T(8,128)}, u32[]{:S(2)}) copy-start(f32[512,12,64]{0,2,1:T(8,128)} %get-tuple-element.403) | copy-start | bytes 4718596
  313.8 3.4 copy-start.38
  317.2 4.8 copy-start.17
  324.3 5.1 copy-start.18
  338.8 4.3 copy-start.3
  338.8 4.3 copy-start.54
  338.8 4.3 copy-start.56
  338.8 4.3 copy-start.58
  338.9 4.3 copy-start.70
  343.2 6.0 copy-start.68
  349.1 110.7 %reduce-scatter.21.cloned.1.call-start = ((), (), s32[]{:S(2)}) async-start(), calls=%async_computation.14 | async-start | bytes 7077888 | tf_op jit(solution)/shard_map/reduce_scatter | solution.py:263
  358.9 163.9 %reduce-scatter.23.cloned.1.call-start = ((), (), s32[]{:S(2)}) async-start(), calls=%async_computation.15 | async-start | bytes 7077888 | tf_op jit(solution)/shard_map/reduce_scatter | solution.py:269
  370.0 180.6 %reduce-scatter.29.cloned.1.call-start = ((), (), s32[]{:S(2)}) async-start(), calls=%async_computation.18 | async-start | bytes 294912
  371.4 9.0 %copy-start.72 = (bf16[768]{0:T(1024)(128)(2,1)S(1)}, bf16[768]{0:T(1024)(128)(2,1)}, u32[]{:S(2)}) copy-start(bf16[768]{0:T(1024)(128)(2,1)} %get-tuple-element.634) | copy-start | bytes 4612
  380.4 7.4 copy-start.64
  386.9 136.0 %copy-start.78 = (u32[32]{0:T(128)S(1)}, u32[32]{0:T(128)}, u32[]{:S(2)}) copy-start(u32[32]{0:T(128)} %constant.209) | copy-start | bytes 388
  386.9 164.6 %reduce-scatter.27.cloned.1.call-start = ((), (), s32[]{:S(2)}) async-start(), calls=%async_computation.17 | async-start | bytes 294912
  387.9 174.5 %reduce-scatter.25.cloned.1.call-start = ((), (), s32[]{:S(2)}) async-start(), calls=%async_computation.16 | async-start | bytes 294912
  388.8 186.6 %reduce-scatter.31.cloned.1.call-start = ((), (), s32[]{:S(2)}) async-start(), calls=%async_computation.19 | async-start | bytes 294912
  389.8 341.9 %all-reduce.5.cloned.1.call-start = ((), (), s32[]{:S(2)}) async-start(), calls=%async_computation.20 | async-start | bytes 14155776 | tf_op jit(solution)/shard_map/psum | solution.py:344
  529.7 3.7 copy-start.10
  529.7 3.7 copy-start.66
  533.4 12.1 %copy-start.65 = (bf16[3072]{0:T(1024)(128)(2,1)S(1)}, bf16[3072]{0:T(1024)(128)(2,1)}, u32[]{:S(2)}) copy-start(bf16[3072]{0:T(1024)(128)(2,1)} %get-tuple-element.638) | copy-start | bytes 18436
  731.6 4.7 copy-start.30
  736.3 4.6 copy-start.48
  (28 other events, 63.0 us)
Sparse Core Ops, SparseCore 0:
  9.6 52.3 all-gather.5
  63.5 22.7 all-gather.7
  87.8 62.6 all-gather.9
  151.9 62.6 all-gather.11
  255.4 21.7 reduce-scatter.18
  349.3 47.6 reduce-scatter.16
  399.8 59.9 reduce-scatter.20
  462.8 60.0 reduce-scatter.22
  525.1 10.9 reduce-scatter.28
  538.2 10.9 reduce-scatter.26
  551.4 10.9 reduce-scatter.24
  564.5 10.9 reduce-scatter.30
  579.5 152.0 all-reduce.4
where the time goes:
time: 759 us; the launch traced here: 749 us
  waiting for transfers between devices  275 us (36%)
  matrix products  241 us (32%)
  blocking collectives  91.8 us (12%)
  other arithmetic  58.7 us (8%)
  local copies, waits for them, and re-layouts  52.9 us (7%)
  between operations  26.3 us (3%)
    psum x1, waiting for transfers between devices, local(): lax.psum(local_grads[2].astype(jnp.bfloat16), 'replica').astype(jnp.float32)  88.3 us
    psum x1, blocking collectives, local(): lax.psum(local_grads[0].astype(jnp.bfloat16), 'replica').astype(jnp.float32)  64 us
    reduce_scatter x1, waiting for transfers between devices, local(): lax.psum_scatter(down_grad.astype(jnp.bfloat16), 'shard', scatter_dimensi...  63 us
    reduce_scatter x1, waiting for transfers between devices, local(): lax.psum_scatter(up_grad.astype(jnp.bfloat16), 'shard', scatter_dimension...  62.9 us
    dot_general x1, matrix products, local(): jnp.dot(normed_two, up_full, preferred_element_type=jnp.float32)  39 us
    dot_general x4, matrix products, spread(): jnp.einsum('hqk,khd->qhd', weights, value_part, preferred_element_type=jn...  33 us
    unnamed x141, local copies, waits for them, and re-layouts  26.3 us
    unnamed x17, waiting for transfers between devices  24.7 us
  transfers between devices with their start and end apart: 13, of which 8 were waited for; matrix products, arithmetic and copies ran while one was open for 39% of the time, Pallas kernels for 0%

commit v1 on v0

v1 whole, which is shorter than its diff:
```python
import functools
import math

import jax
import jax.numpy as jnp
from jax import lax
from jax.experimental import pallas as pl
from jax.experimental.pallas import tpu as pltpu
from jax.sharding import PartitionSpec as P

H = 12
EPS = 1e-05
NEG = -1e30
F32 = jnp.float32
BF = jnp.bfloat16
NN = (((1,), (0,)), ((), ()))
NT = (((1,), (1,)), ((), ()))
TN = (((0,), (0,)), ((), ()))
BLK = 256
GROUPS = 3
VM = pl.BlockSpec(memory_space=pltpu.VMEM)
SM = pl.BlockSpec(memory_space=pltpu.SMEM)
LIMIT = 48 << 20


def mm(a, b, dims=NN):
    return lax.dot_general(a, b, dims, preferred_element_type=F32)


def rows_of(i, size=BLK):
    return pl.ds(pl.multiple_of(i * size, size), size)


def call(kernel, name, outs, n_in, smem, scratch=(), flops=0, moved=0, trans=0):
    return pl.pallas_call(
        kernel,
        name=name,
        out_shape=outs,
        in_specs=[SM] * smem + [VM] * (n_in - smem),
        out_specs=jax.tree.map(lambda _: VM, outs),
        scratch_shapes=list(scratch),
        compiler_params=pltpu.CompilerParams(vmem_limit_bytes=LIMIT),
        cost_estimate=pl.CostEstimate(flops=flops, bytes_accessed=moved, transcendentals=trans),
    )


def array(shape, dtype=BF):
    return jax.ShapeDtypeStruct(shape, dtype)


def standardize(values):
    centered = values - jnp.mean(values, axis=1, keepdims=True)
    inverse = lax.rsqrt(jnp.mean(centered * centered, axis=1, keepdims=True) + EPS)
    return centered * inverse, inverse


def enter_kernel(frames_ref, cot_ref, gain_ref, shift_ref, normed_ref, normedT_ref, sum_ref):
    sum_ref[...] = jnp.zeros_like(sum_ref)

    def step(i, _):
        at = rows_of(i)
        unit, _inv = standardize(frames_ref[at, :].astype(F32))
        normed = (unit * gain_ref[0:1, :] + shift_ref[0:1, :]).astype(BF)
        normed_ref[at, :] = normed
        normedT_ref[:, at] = normed.T
        sum_ref[...] += jnp.sum(cot_ref[at, :].astype(F32), axis=0, keepdims=True)
        return 0

    lax.fori_loop(0, frames_ref.shape[0] // BLK, step, 0)


def enter(frames, cot, gain, shift):
    rows, width = frames.shape
    return call(
        enter_kernel, "enter", (array((rows, width)), array((width, rows)), array((1, width), F32)), 4, 0,
        flops=rows * width * 20, moved=rows * width * 8,
    )(frames, cot, gain, shift)


def windows(seg):
    length = seg.shape[1]
    first = seg[0, ::BLK]
    last = seg[0, BLK - 1 :: BLK]
    begin = jnp.sum((seg < first[:, None]).astype(jnp.int32), axis=1)
    end = jnp.sum((seg <= last[:, None]).astype(jnp.int32), axis=1)
    begin = begin // 16 * 16
    count = (end - begin + BLK - 1) // BLK
    begin = jnp.minimum(begin, length - count * BLK)
    return jnp.stack([begin, count]).astype(jnp.int32)


def by_head(block, dh):
    width = block.shape[1]
    lane = lax.broadcasted_iota(jnp.int32, (1, width), 1) // dh
    zero = jnp.zeros_like(block)
    return jnp.concatenate([jnp.where(lane == h, block, zero) for h in range(width // dh)], axis=0)


def place(full_ref, pos_ref, own_ref, near_ref, far_ref):
    shard, core = pos_ref[0], pos_ref[1]
    size = own_ref.shape[0]
    half = size // 2
    full_ref[pl.ds(pl.multiple_of(shard * size, half), size), :] = own_ref[...]
    for k in range(near_ref.shape[0]):
        base = jnp.bitwise_xor(shard, k + 1) * size
        full_ref[pl.ds(pl.multiple_of(base + core * half, half), half), :] = near_ref[k]
        full_ref[pl.ds(pl.multiple_of(base + (1 - core) * half, half), half), :] = far_ref[k]


def attn_fwd_kernel(dh, pos_ref, win_ref, normed_ref, own_ref, near_ref, far_ref, bias_ref, segr_ref, segc_ref,
                    w_ref, proj_ref, att_ref, attT_ref, lse_ref, acc_ref):
    width = att_ref.shape[1]
    heads = width // dh
    length = normed_ref.shape[0]
    place(w_ref, pos_ref, own_ref, near_ref, far_ref)

    def project(i, _):
        at = rows_of(i)
        proj_ref[at, :] = (mm(normed_ref[at, :], w_ref[...]) + bias_ref[...]).astype(BF)
        return 0

    lax.fori_loop(0, length // BLK, project, 0)

    def queries(step, _):
        at = rows_of(step)
        q = (proj_ref[at, 0:width].astype(F32) * (1.0 / math.sqrt(dh))).astype(BF)
        qall = by_head(q, dh)
        segq = jnp.concatenate([segr_ref[:, at]] * heads, axis=1)
        acc_ref[...] = jnp.zeros_like(acc_ref)
        start = win_ref[0, step]

        def tile(j, carry):
            m_old, mass = carry
            ks = pl.ds(pl.multiple_of(start + j * BLK, 16), BLK)
            vT = proj_ref[ks, 2 * width : 3 * width].T
            same = segc_ref[ks, :] == segq
            s = jnp.where(same, mm(proj_ref[ks, width : 2 * width], qall, NT), NEG)
            m_new = jnp.maximum(m_old, jnp.max(s, axis=0, keepdims=True))
            p = jnp.exp(s - m_new)
            alpha = jnp.exp(m_old - m_new)
            mass = mass * alpha + jnp.sum(p, axis=0, keepdims=True)
            pb = p.astype(BF)
            for h in range(heads):
                hs, cs = slice(h * dh, (h + 1) * dh), slice(h * BLK, (h + 1) * BLK)
                acc_ref[hs, :] = acc_ref[hs, :] * alpha[:, cs] + mm(vT[hs, :], pb[:, cs])
            return m_new, mass

        carry = (jnp.full((1, heads * BLK), NEG, F32), jnp.zeros((1, heads * BLK), F32))
        peak, mass = lax.fori_loop(0, win_ref[1, step], tile, carry)
        lse_ref[:, rows_of(step, heads * BLK)] = peak + jnp.log(mass)
        outs = []
        for h in range(heads):
            outs.append((acc_ref[h * dh : (h + 1) * dh, :] / mass[:, h * BLK : (h + 1) * BLK]).astype(BF))
        oT = jnp.concatenate(outs, axis=0)
        attT_ref[:, at] = oT
        att_ref[at, :] = oT.T
        return 0

    lax.fori_loop(0, length // BLK, queries, 0)


def attn_fwd(dh, pos, win, normed, own, near, far, bias, segr, segc):
    length, d = normed.shape
    width = own.shape[1] // 3
    heads = width // dh
    return call(
        functools.partial(attn_fwd_kernel, dh), "attn_fwd",
        (array((d, 3 * width)), array((length, 3 * width)), array((length, width)), array((width, length)),
         array((1, length * heads), F32)),
        9, 2, [pltpu.VMEM((width, BLK), F32)],
        flops=2 * length * d * 3 * width + 2 * length * length * 256 * heads,
        trans=length * length * heads // 2, moved=length * (d + 6 * width) * 2,
    )(pos, win, normed, own, near, far, bias, segr, segc)


def attn_bwd_kernel(dh, pos_ref, win_ref, proj_ref, att_ref, g_ref, lse_ref, segr_ref, segc_ref, nT_ref,
                    dproj_ref, dw_ref, sums_ref, dk_ref, dv_ref, dqT_ref):
    length, width = att_ref.shape
    heads = width // dh
    scale = 1.0 / math.sqrt(dh)
    dk_ref[...] = jnp.zeros_like(dk_ref)
    dv_ref[...] = jnp.zeros_like(dv_ref)
    row = lax.broadcasted_iota(jnp.int32, (8, width), 0)
    col = lax.broadcasted_iota(jnp.int32, (8, width), 1) // dh
    pick = jnp.where(row == col, 1.0, 0.0).astype(BF)

    def queries(step, _):
        at = rows_of(step)
        q = (proj_ref[at, 0:width].astype(F32) * scale).astype(BF)
        g = g_ref[at, :]
        qall = by_head(q, dh)
        gall = by_head(g, dh)
        og = att_ref[at, :].astype(F32) * g.astype(F32)
        high = og.astype(BF)
        low = (og - high.astype(F32)).astype(BF)
        delta = mm(pick, high, NT) + mm(pick, low, NT)
        delta = jnp.concatenate([delta[h : h + 1, :] for h in range(heads)], axis=1)
        lse = lse_ref[:, rows_of(step, heads * BLK)]
        segq = jnp.concatenate([segr_ref[:, at]] * heads, axis=1)
        dqT_ref[...] = jnp.zeros_like(dqT_ref)
        start = win_ref[0, step]

        def tile(j, _):
            ks = pl.ds(pl.multiple_of(start + j * BLK, 16), BLK)
            kt = proj_ref[ks, width : 2 * width]
            vt = proj_ref[ks, 2 * width : 3 * width]
            kT = kt.T
            same = segc_ref[ks, :] == segq
            p = jnp.where(same, jnp.exp(mm(kt, qall, NT) - lse), 0.0)
            ds = (p * (mm(vt, gall, NT) - delta)).astype(BF)
            dv_ref[ks, :] += mm(p.astype(BF), gall)
            dk_ref[ks, :] += mm(ds, qall)
            for h in range(heads):
                hs = slice(h * dh, (h + 1) * dh)
                dqT_ref[hs, :] += mm(kT[hs, :], ds[:, h * BLK : (h + 1) * BLK])
            return 0

        lax.fori_loop(0, win_ref[1, step], tile, 0)
        dproj_ref[at, 0:width] = (dqT_ref[...] * scale).astype(BF).T
        return 0

    lax.fori_loop(0, length // BLK, queries, 0)
    dproj_ref[:, width : 2 * width] = dk_ref[...].astype(BF)
    dproj_ref[:, 2 * width :] = dv_ref[...].astype(BF)
    sums_ref[...] = jnp.sum(dproj_ref[...].astype(F32), axis=0, keepdims=True)
    piece = dw_ref.shape[1]
    for k in range(dw_ref.shape[0]):
        rs = pl.ds(pl.multiple_of(jnp.bitwise_xor(pos_ref[0], k) * piece, piece), piece)
        dw_ref[k] = mm(nT_ref[rs, :], dproj_ref[...]).astype(BF)


def attn_bwd(dh, pos, win, shards, proj, att, g, lse, segr, segc, nT):
    length, width = att.shape
    d = nT.shape[0]
    heads = width // dh
    return call(
        functools.partial(attn_bwd_kernel, dh), "attn_bwd",
        (array((length, 3 * width)), array((shards, d // shards, 3 * width)), array((1, 3 * width), F32)),
        9, 2, [pltpu.VMEM((length, width), F32), pltpu.VMEM((length, width), F32), pltpu.VMEM((width, BLK), F32)],
        flops=2 * length * d * 3 * width + 5 * length * length * 256 * heads,
        trans=length * length * heads // 2, moved=length * (d + 8 * width) * 2,
    )(pos, win, proj, att, g, lse, segr, segc, nT)


def middle_kernel(pos_ref, frames_ref, a0, a1, a2, own_ref, near_ref, far_ref, outb_ref, gain_ref, shift_ref,
                  w_ref, middle_ref, n_ref, nT_ref):
    place(w_ref, pos_ref, own_ref, near_ref, far_ref)
    width = a0.shape[1]

    def step(i, _):
        at = rows_of(i)
        total = frames_ref[at, :].astype(F32) + outb_ref[0:1, :]
        for g, a in enumerate((a0, a1, a2)):
            total = total + mm(a[at, :], w_ref[g * width : (g + 1) * width, :])
        middle_ref[at, :] = total
        unit, _inv = standardize(total)
        normed = (unit * gain_ref[1:2, :] + shift_ref[1:2, :]).astype(BF)
        n_ref[at, :] = normed
        nT_ref[:, at] = normed.T
        return 0

    lax.fori_loop(0, frames_ref.shape[0] // BLK, step, 0)


def middle(pos, frames, atts, own, near, far, outb, gain, shift):
    rows, d = frames.shape
    return call(
        middle_kernel, "middle",
        (array((d, d)), array((rows, d), F32), array((rows, d)), array((d, rows))), 11, 1,
        flops=2 * rows * d * d, moved=rows * d * 12,
    )(pos, frames, *atts, own, near, far, outb, gain, shift)


def ffn_kernel(own, apart, fresh, offset, step, pos_ref, n_ref, nT_ref, cot_ref, *refs):
    refs = list(refs)
    first, second = refs.pop(0), refs.pop(0)
    if apart:
        first, second = (first, second), (refs.pop(0), refs.pop(0))
    bias_ref = refs.pop(0)
    prev_ref = None if fresh else refs.pop(0)
    act_ref, keep_ref, send_ref, bsum_ref, gn_ref = refs[:5]
    core = pos_ref[1]
    if own:
        up_ref, down_ref = first, second
    else:
        down_ref, up_ref = refs[5], refs[6]
        for ref, t in ((up_ref, 0), (down_ref, 1)):
            size = ref.shape[0] // 2
            ref[pl.ds(pl.multiple_of(core * size, size), size), :] = first[t][...]
            ref[pl.ds(pl.multiple_of((1 - core) * size, size), size), :] = second[t][...]
    d = n_ref.shape[1]
    chunk = act_ref.shape[1]
    gn_ref[...] = jnp.zeros_like(gn_ref) if fresh else prev_ref[...]

    def body(j, _):
        cs = rows_of(j, step)
        ws = pl.ds(pl.multiple_of(offset + j * step, step), step)
        up = up_ref[:, ws]
        hidden = mm(n_ref[...], up) + bias_ref[:, cs]
        grad = mm(cot_ref[...], down_ref[ws, :], NT)
        phi = 0.5 + 0.5 * lax.erf(hidden * (1.0 / math.sqrt(2.0)))
        bell = jnp.exp(hidden * hidden * -0.5) * (1.0 / math.sqrt(2.0 * math.pi))
        act = (hidden * phi).astype(BF)
        gh = (grad * (phi + hidden * bell)).astype(BF)
        act_ref[:, cs] = act
        bsum_ref[:, cs] = jnp.sum(gh.astype(F32), axis=0, keepdims=True)
        gn_ref[...] += mm(gh, up, NT)
        d_down = mm(act, cot_ref[...], TN).astype(BF)
        d_up = mm(nT_ref[...], gh).astype(BF)

        def store(down_to, up_to):
            down_to[cs, :] = d_down
            for r in range(d // chunk):
                at = pl.ds(pl.multiple_of(r * chunk + j * step, step), step)
                up_to[:, at] = d_up[r * chunk : (r + 1) * chunk, :]

        @pl.when(core == 0)
        def _():
            store(keep_ref, send_ref)

        @pl.when(core == 1)
        def _():
            store(send_ref, keep_ref)

        return 0

    lax.fori_loop(0, chunk // step, body, 0)


def ffn(own, offset, pos, n, nT, cot, first, second, bias, grad):
    rows, d = n.shape
    chunk = bias.shape[1]
    step = 256 if chunk % 256 == 0 else 128
    fresh = grad is None
    apart = isinstance(first, tuple)
    args = [pos, n, nT, cot, *(first + second if apart else (first, second)), bias] + ([] if fresh else [grad])
    outs = (array((rows, chunk)), array((chunk, d)), array((chunk, d)), array((1, chunk), F32), array((rows, d), F32))
    if not own:
        outs = outs + (array((chunk, d)),)
    return call(
        functools.partial(ffn_kernel, own, apart, fresh, offset, step), "ffn", outs,
        len(args), 1, [] if own else [pltpu.VMEM((d, chunk), BF)], flops=10 * rows * d * chunk,
        trans=3 * rows * chunk, moved=rows * d * 20,
    )(*args)


def turn_kernel(pos_ref, gn_ref, middle_ref, cot_ref, gain_ref, w_ref, t0, t1, t2,
                gm_ref, g0, g1, g2, dw_ref, sums_ref, branch_ref, mixT_ref):
    width = g0.shape[1]
    sums_ref[...] = jnp.zeros_like(sums_ref)
    for g, t in enumerate((t0, t1, t2)):
        mixT_ref[g * width : (g + 1) * width, :] = t[...]

    def step(i, _):
        at = rows_of(i)
        gn = gn_ref[at, :]
        unit, inverse = standardize(middle_ref[at, :])
        e = gn * gain_ref[1:2, :]
        gm = cot_ref[at, :].astype(F32) + inverse * (
            e - jnp.mean(e, axis=1, keepdims=True) - unit * jnp.mean(e * unit, axis=1, keepdims=True)
        )
        gm_ref[at, :] = gm
        branch = gm.astype(BF)
        branch_ref[at, :] = branch
        sums_ref[0:1, :] += jnp.sum(gn * unit, axis=0, keepdims=True)
        sums_ref[1:2, :] += jnp.sum(gn, axis=0, keepdims=True)
        sums_ref[2:3, :] += jnp.sum(branch.astype(F32), axis=0, keepdims=True)
        for g, out in enumerate((g0, g1, g2)):
            out[at, :] = mm(branch, w_ref[g * width : (g + 1) * width, :], NT).astype(BF)
        return 0

    lax.fori_loop(0, gn_ref.shape[0] // BLK, step, 0)
    piece = dw_ref.shape[1]
    for k in range(dw_ref.shape[0]):
        rs = pl.ds(pl.multiple_of(jnp.bitwise_xor(pos_ref[0], k) * piece, piece), piece)
        dw_ref[k] = mm(mixT_ref[rs, :], branch_ref[...]).astype(BF)


def turn(pos, shards, gn, mid, cot, gain, w, attTs):
    rows, d = gn.shape
    width = d // GROUPS
    return call(
        turn_kernel, "turn",
        (array((rows, d), F32),) + (array((rows, width)),) * 3 + (array((shards, d // shards, d)), array((8, d), F32)),
        9, 1, [pltpu.VMEM((rows, d), BF), pltpu.VMEM((d, rows), BF)],
        flops=4 * rows * d * d, moved=rows * d * 20,
    )(pos, gn, mid, cot, gain, w, *attTs)


def leave_kernel(frames_ref, gm_ref, gain_ref, p0, p1, p2, w0, w1, w2, out_ref, sums_ref):
    sums_ref[...] = jnp.zeros_like(sums_ref)

    def step(i, _):
        at = rows_of(i)
        gn = mm(p0[at, :], w0[...], NT) + mm(p1[at, :], w1[...], NT) + mm(p2[at, :], w2[...], NT)
        unit, inverse = standardize(frames_ref[at, :].astype(F32))
        e = gn * gain_ref[0:1, :]
        out_ref[at, :] = gm_ref[at, :] + inverse * (
            e - jnp.mean(e, axis=1, keepdims=True) - unit * jnp.mean(e * unit, axis=1, keepdims=True)
        )
        sums_ref[0:1, :] += jnp.sum(gn * unit, axis=0, keepdims=True)
        sums_ref[1:2, :] += jnp.sum(gn, axis=0, keepdims=True)
        return 0

    lax.fori_loop(0, frames_ref.shape[0] // BLK, step, 0)


def leave(frames, gm, gain, dprojs, ws):
    rows, d = frames.shape
    return call(
        leave_kernel, "leave", (array((rows, d), F32), array((8, d), F32)), 9, 0,
        flops=6 * rows * d * d, moved=rows * d * 16,
    )(frames, gm, gain, *dprojs, *ws)


def result_kernel(n, offsets, middle_ref, outb_ref, *refs):
    acts, downs, out_ref = refs[:n], refs[n : 2 * n], refs[2 * n]

    def step(i, _):
        at = rows_of(i)
        total = middle_ref[at, :] + outb_ref[1:2, :]
        for a, w, offset in zip(acts, downs, offsets):
            total = total + mm(a[at, :], w[offset : offset + a.shape[1], :])
        out_ref[at, :] = total.astype(BF)
        return 0

    lax.fori_loop(0, middle_ref.shape[0] // BLK, step, 0)


def result(mid, outb, acts, downs, offsets):
    rows, d = mid.shape
    n = len(acts)
    return call(
        functools.partial(result_kernel, n, offsets), "result", array((rows, d)), 2 + 2 * n, 0,
        flops=2 * rows * d * n * acts[0].shape[1], moved=rows * d * 14,
    )(mid, outb, *acts, *downs)


def swap(value, axis, size, bit):
    return lax.ppermute(value, axis, [(i, i ^ bit) for i in range(size)])


def after(value, *others):
    return lax.optimization_barrier((value, *others))[0]


def add(a, b):
    return (a.astype(F32) + b.astype(F32)).astype(a.dtype)


def bits_of(size):
    return [1 << b for b in range(size.bit_length() - 1)]


def spread(own, shards):
    stack = own[None]
    for bit in bits_of(shards):
        stack = jnp.concatenate([stack, swap(stack, "shard", shards, bit)], axis=0)
    return stack


def fetch(half, shards, replicas):
    if shards == 2:
        near = swap(half, "shard", 2, 1)[None]
    else:
        near = spread(half, shards)[1:]
    return near, swap(near, "replica", replicas, 1)


def reduce_shard(pieces, shards):
    for bit in reversed(bits_of(shards)):
        got = swap(jnp.stack(pieces[bit:]) if bit > 1 else pieces[1], "shard", shards, bit)
        pieces = [add(p, got[k] if bit > 1 else got) for k, p in enumerate(pieces[:bit])]
    return pieces[0]


def reduce_replica(total, replicas, which):
    bits = bits_of(replicas)[1:]
    rows = total.shape[0] // 2
    flag = (lax.axis_index("replica") // 2) % 2
    keep = lax.dynamic_slice_in_dim(total, flag * rows, rows, 0)
    send = lax.dynamic_slice_in_dim(total, (1 - flag) * rows, rows, 0)
    part = add(keep, swap(send, "replica", replicas, bits[0]))
    for bit in bits[1:]:
        part = add(part, swap(part, "replica", replicas, bit))
    other = swap(part, "replica", replicas, bits[0])
    full = jnp.where(flag == 0, jnp.concatenate([part, other]), jnp.concatenate([other, part]))
    twin = swap(full, "replica", replicas, 1)
    first = which == 0
    return jnp.where(first, full, twin), jnp.where(first, twin, full)


def natural(stack, shard, axis):
    shards = stack.shape[0]
    shape = list(stack.shape[1:])
    size = shape[axis]
    shape[axis] = size * shards
    out = jnp.zeros(shape, stack.dtype)
    for k in range(shards):
        at = [0] * len(shape)
        at[axis] = (shard ^ k) * size
        out = lax.dynamic_update_slice(out, stack[k], at)
    return out


def pieces_of(value, shards, shard, axis):
    size = value.shape[axis] // shards
    return [lax.dynamic_slice_in_dim(value, (shard ^ k) * size, size, axis) for k in range(shards)]


def local(replicas, shards, frames, cotangent, segment_ids, norm_gain, norm_bias, w_qkv, qv_bias, w_out, out_bias,
          w_up, up_bias, w_down):
    rows, d = frames.shape
    dh = d // H
    group = d // GROUPS
    piece = d // shards
    hid = up_bias.shape[0]
    chunks = max(1, hid // d)
    chunk = hid // chunks
    shard = lax.axis_index("shard")
    replica = lax.axis_index("replica")
    core = replica % 2
    pos = jnp.stack([shard, core]).astype(jnp.int32)

    small = jnp.concatenate([norm_gain, norm_bias, qv_bias, out_bias, up_bias.reshape(-1, piece)], axis=0)
    smalls = spread(small, shards)
    whole = natural(smalls[:, :8], shard, 1).astype(F32)
    gain, shift, qv, outb = whole[0:2], whole[2:4], whole[4:6], whole[6:8]
    up_bias_all = smalls[:, 8:].reshape(shards, 1, hid).astype(F32)

    half = piece // 2
    mine = lax.dynamic_slice_in_dim(w_qkv, core * half, half, 0).reshape(half, 3, GROUPS, group)
    own_qkv = w_qkv.reshape(piece, 3, GROUPS, group)
    qkv_halves = [mine[:, :, g].reshape(half, 3 * group) for g in range(GROUPS)]
    qkv_own = [own_qkv[:, :, g].reshape(piece, 3 * group) for g in range(GROUPS)]
    out_half = lax.dynamic_slice_in_dim(w_out, core * half, half, 0)
    up_half = lax.dynamic_slice_in_dim(w_up, core * (d // 2), d // 2, 0)
    down_half = lax.dynamic_slice_in_dim(w_down.reshape(chunks, 2, chunk // 2, d), core, 1, 1)
    fetched = []
    sends = list(qkv_halves) + [out_half]
    for i in range(chunks):
        up_part = up_half[:, i * chunk : (i + 1) * chunk]
        if chunk == d:
            sends.append(jnp.stack([up_part, down_half[i, 0]]))
        else:
            sends.append((up_part, down_half[i, 0]))
    for i, send in enumerate(sends):
        if i:
            send = after(send, fetched[max(0, i - 2)][0])
        if isinstance(send, tuple):
            a, b = [fetch(v, shards, replicas) for v in send]
            fetched.append(((a[0], b[0]), (a[1], b[1])))
        else:
            fetched.append(fetch(send, shards, replicas))

    win = windows(segment_ids)
    segc = segment_ids.reshape(rows, 1)
    normed, normedT, cot_sum = enter(frames, cotangent, gain, shift)
    zero = jnp.zeros((1, group), F32)
    ws, projs, atts, attTs, lses = [], [], [], [], []
    for g in range(GROUPS):
        cols = slice(g * group, (g + 1) * group)
        bias = jnp.concatenate([qv[0:1, cols], zero, qv[1:2, cols]], axis=1)
        w, proj, att, attT, lse = attn_fwd(dh, pos, win, normed, qkv_own[g], *fetched[g], bias, segment_ids, segc)
        ws.append(w)
        projs.append(proj)
        atts.append(att)
        attTs.append(attT)
        lses.append(lse)
    w_out_all, mid, n_two, nT_two = middle(pos, frames, atts, w_out, *fetched[GROUPS], outb, gain, shift)

    grad, acts, downs, offsets = None, [], [], []
    keeps = [[None] * chunks for _ in range(shards)]
    got = [[None] * chunks for _ in range(shards)]
    up_sums = [[None] * chunks for _ in range(shards)]
    for k in range(shards):
        for i in range(chunks):
            bias = up_bias_all[k, :, i * chunk : (i + 1) * chunk]
            if k == 0:
                out = ffn(True, i * chunk, pos, n_two, nT_two, cotangent, w_up, w_down, bias, grad)
                downs.append(w_down)
                offsets.append(i * chunk)
            else:
                near, far = fetched[GROUPS + 1 + i]
                if isinstance(near, tuple):
                    near = near[0][k - 1], near[1][k - 1]
                    far = far[0][k - 1], far[1][k - 1]
                    out = ffn(False, 0, pos, n_two, nT_two, cotangent, near, far, bias, grad)
                else:
                    out = ffn(False, 0, pos, n_two, nT_two, cotangent, near[k - 1], far[k - 1], bias, grad)
                downs.append(out[5])
                offsets.append(0)
            acts.append(out[0])
            keeps[k][i] = out[1]
            got[k][i] = swap(out[2], "replica", replicas, 1)
            up_sums[k][i] = out[3]
            grad = out[4]
    ffn_grads = []
    for i in range(chunks):
        sums = [add(keeps[k][i], got[k][i]) for k in range(shards)]
        ffn_grads.append(reduce_replica(reduce_shard(sums, shards), replicas, core))

    out = turn(pos, shards, grad, mid, cotangent, gain, w_out_all, attTs)
    gm, gs, d_out, sums_two = out[0], out[1:4], out[4], out[5]
    dprojs, dws, qv_sums = [], [], []
    for g in range(GROUPS):
        dproj, dw, sums = attn_bwd(dh, pos, win, shards, projs[g], atts[g], gs[g], lses[g], segment_ids, segc, normedT)
        dprojs.append(dproj)
        dws.append(dw)
        qv_sums.append(sums)
    d_frames, sums_one = leave(frames, gm, gain, dprojs, ws)
    attn_grads = []
    for a, b in ((d_out, dws[0]), (dws[1], dws[2])):
        keep = jnp.where(core == 0, a, b)
        send = jnp.where(core == 0, b, a)
        both = add(keep, swap(send, "replica", replicas, 1))
        attn_grads.append(reduce_replica(reduce_shard([both[k] for k in range(shards)], shards), replicas, core))

    qv_sum = jnp.concatenate(qv_sums, axis=0)
    tall = jnp.concatenate(
        [sums_one[0:1], sums_two[0:1], sums_one[1:2], sums_two[1:2], qv_sum[:, :group].reshape(1, d),
         qv_sum[:, 2 * group :].reshape(1, d), sums_two[2:3], cot_sum], axis=0)
    parts = pieces_of(tall, shards, shard, 1)
    parts = [jnp.concatenate([p.reshape(-1), *[u.reshape(-1) for u in up_sums[k]]]).reshape(-1, piece) for k, p in enumerate(parts)]
    vec = reduce_shard(parts, shards)
    for bit in bits_of(replicas):
        vec = add(vec, swap(vec, "replica", replicas, bit))

    out_frames = result(mid, outb, acts, downs, tuple(offsets))

    d_down = jnp.concatenate([c[0] for c in ffn_grads], axis=0).astype(F32)
    ups = []
    for c in ffn_grads:
        up = c[1]
        ups.append(jnp.concatenate([up[:, r * chunk : (r + 1) * chunk] for r in range(d // chunk)], axis=0))
    d_up = jnp.concatenate(ups, axis=1).astype(F32)
    d_wout = attn_grads[0][0].astype(F32)
    groups = [attn_grads[0][1], attn_grads[1][0], attn_grads[1][1]]
    d_qkv = jnp.concatenate([g[:, t * group : (t + 1) * group] for t in range(3) for g in groups], axis=1).astype(F32)
    return (
        out_frames, d_frames, vec[0:2], vec[2:4], d_qkv, vec[4:6], d_wout, vec[6:8], d_up,
        vec[8:].reshape(hid), d_down,
    )


def solution(mesh):
    both = P(("replica", "shard"), None)
    wide, tall, flat = P(None, "shard"), P("shard", None), P("shard")
    return jax.shard_map(
        functools.partial(local, mesh.shape["replica"], mesh.shape["shard"]),
        mesh=mesh,
        in_specs=(both, both, both, wide, wide, tall, wide, tall, wide, wide, flat, tall),
        out_specs=(both, both, wide, wide, tall, wide, tall, wide, wide, flat, tall),
        check_vma=False,
    )
```

time: 759 us -> 517 us (0.68)
  matrix products: 241 us -> 0 us
  Pallas kernels: 0 us -> 185 us
  waiting for transfers between devices: 275 us -> 172 us
  blocking collectives: 91.8 us -> 0 us
  starting transfers between devices: 0.99 us -> 42.9 us
  other arithmetic: 58.7 us -> 32.4 us
  between operations: 26.3 us -> 2.22 us
  local copies, waits for them, and re-layouts: 52.9 us -> 72.3 us
    dot_general x40 -> x0, matrix products: 241 us -> none  [the longest x1 39 us: local(): jnp.dot(normed_two, up_full, preferred_element_type=jnp.float32)]
    pallas_call x0 -> x15, Pallas kernels: none -> 185 us  [the longest x4 61 us: ffn(): call(functools.partial(ffn_kernel, own, apart, fresh, offset, step), 'ffn...]
    ppermute x0 -> x48, waiting for transfers between devices: none -> 172 us  [swap(): return lax.ppermute(value, axis, [(i, i ^ bit) for i in range(size)])]
    reduce_scatter x4 -> x0, waiting for transfers between devices: 133 us -> none  [the longest x1 63 us: local(): lax.psum_scatter(down_grad.astype(jnp.bfloat16), 'shard', scatter_dimensi...]
    psum x1 -> x0, waiting for transfers between devices: 88.3 us -> none  [local(): lax.psum(local_grads[2].astype(jnp.bfloat16), 'replica').astype(jnp.float32)]
    psum x1 -> x0, blocking collectives: 64 us -> none  [local(): lax.psum(local_grads[0].astype(jnp.bfloat16), 'replica').astype(jnp.float32)]
    ppermute x0 -> x48, starting transfers between devices: none -> 42.9 us  [swap(): return lax.ppermute(value, axis, [(i, i ^ bit) for i in range(size)])]
    all_gather x4 -> x0, waiting for transfers between devices: 29.4 us -> none  [the longest x1 16.4 us: local(): lax.all_gather(w_down, 'shard', axis=0, tiled=True)]
  transfers between devices with their start and end apart: 13 -> 48, of which waited for: 8 -> 21; matrix products, arithmetic and copies ran while one was open for 39% -> 10% of each run, Pallas kernels for 0% -> 36%
where the time goes in v1:
time: 517 us; the launch traced here: 507 us
  Pallas kernels  185 us (36%)
  waiting for transfers between devices  172 us (33%)
  local copies, waits for them, and re-layouts  72.3 us (14%)
  starting transfers between devices  42.9 us (8%)
  other arithmetic  32.4 us (6%)
    ppermute x48, waiting for transfers between devices, swap(): return lax.ppermute(value, axis, [(i, i ^ bit) for i in range(size)])  172 us
    pallas_call x4, Pallas kernels, ffn(): call(functools.partial(ffn_kernel, own, apart, fresh, offset, step), 'ffn...  61 us
    unnamed x208, local copies, waits for them, and re-layouts  46.2 us
    pallas_call x3, Pallas kernels, attn_bwd(): call(functools.partial(attn_bwd_kernel, dh), 'attn_bwd', (array((length,...  44.9 us
    ppermute x48, starting transfers between devices, swap(): return lax.ppermute(value, axis, [(i, i ^ bit) for i in range(size)])  42.9 us
    pallas_call x3, Pallas kernels, attn_fwd(): call(functools.partial(attn_fwd_kernel, dh), 'attn_fwd', (array((d, 3 * w...  36.8 us
    pallas_call x1, Pallas kernels, result(): call(functools.partial(result_kernel, n, offsets), 'result', array((rows,...  11.3 us
    pallas_call x1, Pallas kernels, leave(): call(leave_kernel, 'leave', (array((rows, d), F32), array((8, d), F32)),...  10.6 us
  transfers between devices with their start and end apart: 48, of which 21 were waited for; matrix products, arithmetic and copies ran while one was open for 10% of the time, Pallas kernels for 36%

profile of v1, /device:TPU:0, one launch (start us, length us, event | category | flops | bytes accessed | tf_op | source)
XLA Modules:
  0.0 507.0 jit_solution(17086248868671587287)
XLA Ops:
  2.4 4.7 slice_reduce_fusion
  7.8 3.0 collective-permute-start.1
  11.2 2.8 copy.36
  15.6 1.5 dynamic-slice_bitcast_fusion.1
  23.6 2.3 copy.39.own_ref
  27.0 2.1 collective-permute-start.3
  29.7 7.6 %collective-permute-done.3 = bf16[192,768]{1,0:T(8,128)(2,1)} collective-permute-done((bf16[192,768]{1,0:T(8,128)(2,1)}, bf16[192,768]{1,0:T(8,128)(2,1)}, u32[]{:S(2)}, u32[]{:S(2)}) %collective-permute-start.3) | collective-permute-done | bytes 294944 | tf_op jit(solution)/shard_map/ppermute | solution.py:440
  37.3 2.0 collective-permute-start.7
  39.4 4.1 collective-permute-done.5
  43.5 2.0 collective-permute-start.9
  45.5 4.3 collective-permute-done.7
  49.8 2.0 collective-permute-start.11
  51.9 3.3 enter.1
  59.1 12.2 %attn_fwd.3 = (bf16[768,768]{1,0:T(8,128)(2,1)S(1)}, bf16[1024,768]{1,0:T(8,128)(2,1)S(1)}, bf16[1024,256]{1,0:T(8,128)(2,1)S(1)}, bf16[256,1024]{1,0:T(8,128)(2,1)S(1)}, f32[1,4096]{1,0:T(1,128)S(1)}) custom-call(s32[2]{0:T(128)S(1)} %pad_add_fusion.1.pos_ref, s32[2,4]{1,0:T(2,128)S(1)} %pad_add_fusion.win_ref, bf16[1024,768]{1,0:T(8,128)(2,1)} %copy-done.51, ...), custom_call_target="tpu_custom_call" | custom-call | flops 3355443200 | bytes 4718592 | tf_op jit(solution)/shard_map/attn_fwd/pallas_call | solution.py:166
  74.4 12.3 %attn_fwd.5 = (bf16[768,768]{1,0:T(8,128)(2,1)S(1)}, bf16[1024,768]{1,0:T(8,128)(2,1)S(1)}, bf16[1024,256]{1,0:T(8,128)(2,1)S(1)}, bf16[256,1024]{1,0:T(8,128)(2,1)S(1)}, f32[1,4096]{1,0:T(1,128)S(1)}) custom-call(s32[2]{0:T(128)S(1)} %pad_add_fusion.1.pos_ref, s32[2,4]{1,0:T(2,128)S(1)} %pad_add_fusion.win_ref, bf16[1024,768]{1,0:T(8,128)(2,1)} %copy-done.51, ...), custom_call_target="tpu_custom_call" | custom-call | flops 3355443200 | bytes 4718592 | tf_op jit(solution)/shard_map/attn_fwd/pallas_call | solution.py:166
  91.7 12.2 %attn_fwd.4 = (bf16[768,768]{1,0:T(8,128)(2,1)S(1)}, bf16[1024,768]{1,0:T(8,128)(2,1)S(1)}, bf16[1024,256]{1,0:T(8,128)(2,1)S(1)}, bf16[256,1024]{1,0:T(8,128)(2,1)S(1)}, f32[1,4096]{1,0:T(1,128)S(1)}) custom-call(s32[2]{0:T(128)S(1)} %copy-done.46, s32[2,4]{1,0:T(2,128)S(1)} %copy-done.43, bf16[1024,768]{1,0:T(8,128)(2,1)} %copy-done.51, ...), custom_call_target="tpu_custom_call" | custom-call | flops 3355443200 | bytes 4718592 | tf_op jit(solution)/shard_map/attn_fwd/pallas_call | solution.py:166
  107.7 7.1 %middle.1 = (bf16[768,768]{1,0:T(8,128)(2,1)S(1)}, f32[1024,768]{1,0:T(8,128)}, bf16[1024,768]{1,0:T(8,128)(2,1)S(1)}, bf16[768,1024]{1,0:T(8,128)(2,1)}) custom-call(s32[2]{0:T(128)S(1)} %copy-done.46, bf16[1024,768]{1,0:T(8,128)(2,1)} %frames_ref.5, bf16[1024,256]{1,0:T(8,128)(2,1)S(1)} %get-tuple-element.78.a0.att_ref, ...), custom_call_target="tpu_custom_call" | custom-call | flops 1207959552 | bytes 9437184 | tf_op jit(solution)/shard_map/middle/pallas_call | solution.py:267
  116.2 14.4 %ffn.4 = (bf16[1024,768]{1,0:T(8,128)(2,1)S(1)}, bf16[768,768]{1,0:T(8,128)(2,1)S(1)}, bf16[768,768]{1,0:T(8,128)(2,1)S(1)}, f32[1,768]{1,0:T(1,128)S(1)}, f32[1024,768]{1,0:T(8,128)}) custom-call(s32[2]{0:T(128)S(1)} %copy-done.46, bf16[1024,768]{1,0:T(8,128)(2,1)S(1)} %get-tuple-element.85.n_ref, bf16[768,1024]{1,0:T(8,128)(2,1)} %get-tuple-element.86.nT_ref, ...), custom_call_target="tpu_custom_call" | custom-call | flops 6039797760 | bytes 15728640 | tf_op jit(solution)/shard_map/ffn/pallas_call | solution.py:340
  133.8 15.1 %ffn.5 = (bf16[1024,768]{1,0:T(8,128)(2,1)S(1)}, bf16[768,768]{1,0:T(8,128)(2,1)S(1)}, bf16[768,768]{1,0:T(8,128)(2,1)S(1)}, f32[1,768]{1,0:T(1,128)S(1)}, f32[1024,768]{1,0:T(8,128)}) custom-call(s32[2]{0:T(128)S(1)} %copy-done.46, bf16[1024,768]{1,0:T(8,128)(2,1)S(1)} %get-tuple-element.85.n_ref, bf16[768,1024]{1,0:T(8,128)(2,1)} %get-tuple-element.86.nT_ref, ...), custom_call_target="tpu_custom_call" | custom-call | flops 6039797760 | bytes 15728640 | tf_op jit(solution)/shard_map/ffn/pallas_call | solution.py:340
  154.7 15.9 %ffn.6 = (bf16[1024,768]{1,0:T(8,128)(2,1)}, bf16[768,768]{1,0:T(8,128)(2,1)S(1)}, bf16[768,768]{1,0:T(8,128)(2,1)}, f32[1,768]{1,0:T(1,128)S(1)}, f32[1024,768]{1,0:T(8,128)}, /*index=5*/bf16[768,768]{1,0:T(8,128)(2,1)S(1)}) custom-call(s32[2]{0:T(128)S(1)} %copy-done.47, bf16[1024,768]{1,0:T(8,128)(2,1)} %copy-done.59, ...), custom_call_target="tpu_custom_call" | custom-call | flops 6039797760 | bytes 15728640 | tf_op jit(solution)/shard_map/ffn/pallas_call | solution.py:340
  173.6 1.3 reduce.5
  176.2 15.6 %ffn.7 = (bf16[1024,768]{1,0:T(8,128)(2,1)}, bf16[768,768]{1,0:T(8,128)(2,1)S(1)}, bf16[768,768]{1,0:T(8,128)(2,1)S(1)}, f32[1,768]{1,0:T(1,128)S(1)}, f32[1024,...) custom-call(s32[2]{0:T(128)S(1)} %copy-done.48, bf16[1024,768]{1,0:T(8,128)(2,1)} %copy-done.59, ...), custom_call_target="tpu_custom_call" | custom-call | flops 6039797760 | bytes 15728640 | tf_op jit(solution)/shard_map/ffn/pallas_call | solution.py:340
  195.2 9.5 %turn.1 = (f32[1024,768]{1,0:T(8,128)}, bf16[1024,256]{1,0:T(8,128)(2,1)S(1)}, bf16[1024,256]{1,0:T(8,128)(2,1)S(1)}, bf16[1024,256]{1,0:T(8,128)(2,1)S(1)}, bf1...) custom-call(s32[2]{0:T(128)S(1)} %copy-done.48, f32[1024,768]{1,0:T(8,128)} %get-tuple-element.98.gn_ref, ...), custom_call_target="tpu_custom_call" | custom-call | flops 2415919104 | bytes 15728640 | tf_op jit(solution)/shard_map/turn/pallas_call | solution.py:382
  204.7 15.1 %attn_bwd.5 = (bf16[1024,768]{1,0:T(8,128)(2,1)S(1)}, bf16[2,384,768]{2,1,0:T(8,128)(2,1)S(1)}, f32[1,768]{1,0:T(1,128)S(1)}) custom-call(s32[2]{0:T(128)S(1)} %copy-done.49, s32[2,4]{1,0:T(2,128)S(1)} %copy-done.44, bf16[1024,768]{1,0:T(8,128)(2,1)S(1)} %copy-done.78, bf16[1024,256]{1,0:T(8,128)(2,1)S(1)} %copy-done.63, ...), custom_call_target="tpu_custom_call" | custom-call | flops 6576668672 | bytes 5767168 | tf_op jit(solution)/shard_map/attn_bwd/pallas_call | solution.py:236
  221.0 14.8 %attn_bwd.4 = (bf16[1024,768]{1,0:T(8,128)(2,1)S(1)}, bf16[2,384,768]{2,1,0:T(8,128)(2,1)S(1)}, f32[1,768]{1,0:T(1,128)S(1)}) custom-call(s32[2]{0:T(128)S(1)} %copy-done.49, s32[2,4]{1,0:T(2,128)S(1)} %copy-done.44, bf16[1024,768]{1,0:T(8,128)(2,1)S(1)} %copy-done.80, bf16[1024,256]{1,0:T(8,128)(2,1)S(1)} %copy-done.65, ...), custom_call_target="tpu_custom_call" | custom-call | flops 6576668672 | bytes 5767168 | tf_op jit(solution)/shard_map/attn_bwd/pallas_call | solution.py:236
  238.5 15.1 %attn_bwd.3 = (bf16[1024,768]{1,0:T(8,128)(2,1)S(1)}, bf16[2,384,768]{2,1,0:T(8,128)(2,1)S(1)}, f32[1,768]{1,0:T(1,128)S(1)}) custom-call(s32[2]{0:T(128)S(1)} %copy-done.49, s32[2,4]{1,0:T(2,128)S(1)} %copy-done.44, bf16[1024,768]{1,0:T(8,128)(2,1)S(1)} %copy-done.76, bf16[1024,256]{1,0:T(8,128)(2,1)S(1)} %copy-done.61, ...), custom_call_target="tpu_custom_call" | custom-call | flops 6576668672 | bytes 5767168 | tf_op jit(solution)/shard_map/attn_bwd/pallas_call | solution.py:236
  255.7 10.6 %leave.1 = (f32[1024,768]{1,0:T(8,128)}, f32[8,768]{1,0:T(8,128)S(1)}) custom-call(bf16[1024,768]{1,0:T(8,128)(2,1)S(1)} %copy-done.3, f32[1024,768]{1,0:T(8,128)} %get-tuple-element.103.gm_ref, f32[2,768]{1,0:T(2,128)S(1)} %get-tuple-element.180.gain_ref, bf16[1024,768]{1,0:T(8,128)(2,1)} %copy-done.68, bf16[1024,768]{1,0:T(8,128)(2,1)} %copy-done.67, ...), custom_call_target="tpu_custom_call" | custom-call | flops 3623878656 | bytes 12582912 | tf_op jit(solution)/shard_map/leave/pallas_call | solution.py:410
  268.7 1.4 concatenate.66
  270.1 1.3 constant_dynamic-slice_fusion.4
  271.4 1.3 reshape.226
  273.4 1.3 pad_maximum_fusion.3
  274.7 1.3 reshape.229
  276.1 1.3 reshape.222
  277.4 1.3 pad_maximum_fusion.2
  278.7 1.3 reshape.225
  282.8 1.8 collective-permute-start.15
  284.6 2.3 collective-permute-done.15
  287.7 1.9 collective-permute-start.16
  289.6 1.6 broadcast_select_fusion.5
  291.5 2.5 collective-permute-start.17
  296.6 11.3 %result.1 = bf16[1024,768]{1,0:T(8,128)(2,1)} custom-call(f32[1024,768]{1,0:T(8,128)} %get-tuple-element.84.middle_ref, f32[2,768]{1,0:T(2,128)S(1)} %get-tuple-element.178.outb_ref, bf16[1024,768]{1,0:T(8,128)(2,1)S(1)} %copy-done.5, bf16[1024,768]{1,0:T(8,128)(2,1)S(1)} %copy-done.7, bf16[1024,768]{1,0:T(8,128)(2,1)} %get-tuple-element.92.refs_2_, ...), custom_call_target="tpu_custom_call" | custom-call | flops 4831838208 | bytes 11010048 | tf_op jit(solution)/shard_map/result/pallas_call | solution.py:433
  308.5 1.6 add_convert_fusion.4
  310.1 1.6 collective-permute-start.34
  311.7 1.8 add_convert_fusion.6
  316.8 34.8 %collective-permute-done.26 = bf16[384,768]{1,0:T(8,128)(2,1)S(1)} collective-permute-done((bf16[384,768]{1,0:T(8,128)(2,1)S(1)}, bf16[384,768]{1,0:T(8,128)(2,1)S(1)}, u32[]{:S(2)}, u32[]{:S(2)}) %collective-permute-start.26) | collective-permute-done | bytes 589856 | tf_op jit(solution)/shard_map/ppermute | solution.py:440
  351.6 1.5 collective-permute-start.42
  353.4 10.9 %collective-permute-done.19 = bf16[384,768]{1,0:T(8,128)(2,1)S(1)} collective-permute-done((bf16[384,768]{1,0:T(8,128)(2,1)S(1)}, bf16[384,768]{1,0:T(8,128)(2,1)S(1)}, u32[]{:S(2)}, u32[]{:S(2)}) %collective-permute-start.19) | collective-permute-done | bytes 589856 | tf_op jit(solution)/shard_map/ppermute | solution.py:440
  368.4 5.8 %collective-permute-done.27 = bf16[192,768]{1,0:T(8,128)(2,1)S(1)} collective-permute-done((bf16[192,768]{1,0:T(8,128)(2,1)S(1)}, bf16[192,768]{1,0:T(8,128)(2,1)S(1)}, u32[]{:S(2)}, u32[]{:S(2)}) %collective-permute-start.27) | collective-permute-done | bytes 294944 | tf_op jit(solution)/shard_map/ppermute | solution.py:440
  374.3 2.1 collective-permute-start.28
  376.4 4.1 collective-permute-done.20
  380.6 2.1 collective-permute-start.21
  382.8 6.1 %collective-permute-done.42 = bf16[768,768]{1,0:T(8,128)(2,1)S(1)} collective-permute-done((bf16[768,768]{1,0:T(8,128)(2,1)S(1)}, bf16[768,768]{1,0:T(8,128)(2,1)S(1)}, u32[]{:S(2)}, u32[]{:S(2)}) %collective-permute-start.42) | collective-permute-done | bytes 1179680 | tf_op jit(solution)/shard_map/ppermute | solution.py:440
  391.8 1.9 collective-permute-start.22
  393.8 1.9 collective-permute-start.36
  395.7 17.7 %collective-permute-done.29 = bf16[192,768]{1,0:T(8,128)(2,1)S(1)} collective-permute-done((bf16[192,768]{1,0:T(8,128)(2,1)S(1)}, bf16[192,768]{1,0:T(8,128)(2,1)S(1)}, u32[]{:S(2)}, u32[]{:S(2)}) %collective-permute-start.29) | collective-permute-done | bytes 294944 | tf_op jit(solution)/shard_map/ppermute | solution.py:440
  414.6 3.7 collective-permute-done.22
  421.1 5.5 %collective-permute-done.23 = bf16[192,768]{1,0:T(8,128)(2,1)S(1)} collective-permute-done((bf16[192,768]{1,0:T(8,128)(2,1)S(1)}, bf16[192,768]{1,0:T(8,128)(2,1)S(1)}, u32[]{:S(2)}, u32[]{:S(2)}) %collective-permute-start.23) | collective-permute-done | bytes 294944 | tf_op jit(solution)/shard_map/ppermute | solution.py:440
  428.9 6.7 %collective-permute-done.44 = bf16[384,768]{1,0:T(8,128)(2,1)} collective-permute-done((bf16[384,768]{1,0:T(8,128)(2,1)S(1)}, bf16[384,768]{1,0:T(8,128)(2,1)}, u32[]{:S(2)}, u32[]{:S(2)}) %collective-permute-start.44) | collective-permute-done | bytes 589856 | tf_op jit(solution)/shard_map/ppermute | solution.py:440
  438.6 32.7 %collective-permute-done.37 = bf16[384,768]{1,0:T(8,128)(2,1)S(1)} collective-permute-done((bf16[384,768]{1,0:T(8,128)(2,1)S(1)}, bf16[384,768]{1,0:T(8,128)(2,1)S(1)}, u32[]{:S(2)}, u32[]{:S(2)}) %collective-permute-start.37) | collective-permute-done | bytes 589856 | tf_op jit(solution)/shard_map/ppermute | solution.py:440
  472.0 11.0 %collective-permute-done.45 = bf16[384,768]{1,0:T(8,128)(2,1)S(1)} collective-permute-done((bf16[384,768]{1,0:T(8,128)(2,1)S(1)}, bf16[384,768]{1,0:T(8,128)(2,1)S(1)}, u32[]{:S(2)}, u32[]{:S(2)}) %collective-permute-start.45) | collective-permute-done | bytes 589856 | tf_op jit(solution)/shard_map/ppermute | solution.py:440
  485.5 12.1 %collective-permute-done.46 = bf16[384,768]{1,0:T(8,128)(2,1)S(1)} collective-permute-done((bf16[384,768]{1,0:T(8,128)(2,1)S(1)}, bf16[384,768]{1,0:T(8,128)(2,1)S(1)}, u32[]{:S(2)}, u32[]{:S(2)}) %collective-permute-start.46) | collective-permute-done | bytes 589856 | tf_op jit(solution)/shard_map/ppermute | solution.py:440
  498.3 2.0 convert_element_type.276
  501.2 2.5 maximum_convert_fusion.1
  503.7 2.8 maximum_convert_fusion
  (350 shorter events, 86.7 us)
Async XLA Ops:
  7.8 19.2 %collective-permute-start.1 = (bf16[192,768]{1,0:T(8,128)(2,1)}, bf16[192,768]{1,0:T(8,128)(2,1)S(1)}, u32[]{:S(2)}, u32[]{:S(2)}) collective-permute-start(bf16[192,768]{1,0:T(8,128)(2,1)} %bitcast.39), channel_id=1, source_target_pairs={{0,1},{1,0},{2,3},{3,2},{4,5},{5,4},{6,7},{7,6},{8,9},{9,8},{10,11... | collective-permute-start | bytes 884744 | tf_op jit(solution)/shard_map/ppermute | solution.py:440
  10.9 18.2 %collective-permute-start = (bf16[1,12,384]{2,1,0:T(8,128)(2,1)S(1)}, bf16[1,12,384]{2,1,0:T(8,128)(2,1)S(1)}, u32[]{:S(2)}, u32[]{:S(2)}) collective-permute-start(bf16[1,12,384]{2,1,0:T(8,128)(2,1)S(1)} %bitcast.114), channel_id=1, source_target_pairs={{0,1},{1,0},{2,3},{3,2},{4,5},{5,4},{6,7},{7,6},{8,9},{9,8},{10,11... | collective-permute-start | bytes 27656 | tf_op jit(solution)/shard_map/ppermute | solution.py:440
  18.8 55.5 %copy-start.42 = (s32[2,4]{1,0:T(2,128)}, s32[2,4]{1,0:T(2,128)S(1)}, u32[]{:S(2)}) copy-start(s32[2,4]{1,0:T(2,128)S(1)} %pad_add_fusion.win_ref) | copy-start | bytes 100
  20.0 54.3 %copy-start.45 = (s32[2]{0:T(128)}, s32[2]{0:T(128)S(1)}, u32[]{:S(2)}) copy-start(s32[2]{0:T(128)S(1)} %pad_add_fusion.1.pos_ref) | copy-start | bytes 28
  23.6 28.2 %copy-start.2 = (bf16[1024,768]{1,0:T(8,128)(2,1)S(1)}, bf16[1024,768]{1,0:T(8,128)(2,1)}, u32[]{:S(2)}) copy-start(bf16[1024,768]{1,0:T(8,128)(2,1)} %frames_ref.5) | copy-start | bytes 4718596
  27.0 28.3 %copy-start.57 = (bf16[192,768]{1,0:T(8,128)(2,1)}, bf16[192,768]{1,0:T(8,128)(2,1)S(1)}, u32[]{:S(2)}) copy-start(bf16[192,768]{1,0:T(8,128)(2,1)S(1)} %collective-permute-done.1) | copy-start | bytes 884740
  27.0 10.3 %collective-permute-start.3 = (bf16[192,768]{1,0:T(8,128)(2,1)}, bf16[192,768]{1,0:T(8,128)(2,1)}, u32[]{:S(2)}, u32[]{:S(2)}) collective-permute-start(bf16[192,768]{1,0:T(8,128)(2,1)} %bitcast.113), channel_id=1, source_target_pairs={{0,1},{1,0},{2,3},{3,2},{4,5},{5,4},{6,7},{7,6},{8,9},{9,8},{10,11... | collective-permute-start | bytes 884744 | tf_op jit(solution)/shard_map/ppermute | solution.py:440
  29.7 13.8 %collective-permute-start.5 = (bf16[192,768]{1,0:T(8,128)(2,1)S(1)}, bf16[192,768]{1,0:T(8,128)(2,1)S(1)}, u32[]{:S(2)}, u32[]{:S(2)}) collective-permute-start(bf16[192,768]{1,0:T(8,128)(2,1)S(1)} %bitcast.112), channel_id=1, source_target_pairs={{0,1},{1,0},{2,3},{3,2},{4,5},{5,4},{6,7},{7,6},{8,9},{9,8},{10,11... | collective-permute-start | bytes 884744 | tf_op jit(solution)/shard_map/ppermute | solution.py:440
  37.3 12.5 %collective-permute-start.7 = (bf16[192,768]{1,0:T(8,128)(2,1)S(1)}, bf16[192,768]{1,0:T(8,128)(2,1)S(1)}, u32[]{:S(2)}, u32[]{:S(2)}) collective-permute-start(bf16[192,768]{1,0:T(8,128)(2,1)S(1)} %constant_dynamic-slice_fusion.6), channel_id=1, source_target_pairs={{0,1},{1,0},{2,3},{3,2},{4,5},{5,4},{6,7},{7,6},{8,9},{9,8},{10,11... | collective-permute-start | bytes 884744 | tf_op jit(solution)/shard_map/ppermute | solution.py:440
  39.3 18.8 %collective-permute-start.2 = (bf16[1,192,768]{2,1,0:T(8,128)(2,1)S(1)}, bf16[1,192,768]{2,1,0:T(8,128)(2,1)S(1)}, u32[]{:S(2)}, u32[]{:S(2)}) collective-permute-start(bf16[1,192,768]{2,1,0:T(8,128)(2,1)S(1)} %bitcast.98), channel_id=1, source_target_pairs={{0,2},{2,0},{4,6},{6,4},{8,10},{10,8},{12,14},{14,12},{16,18},{18,... | collective-permute-start | bytes 884744 | tf_op jit(solution)/shard_map/ppermute | solution.py:440
  43.5 64.1 %collective-permute-start.9 = (bf16[2,384,768]{2,1,0:T(8,128)(2,1)}, bf16[2,384,768]{2,1,0:T(8,128)(2,1)}, u32[]{:S(2)}, u32[]{:S(2)}) collective-permute-start(bf16[2,384,768]{2,1,0:T(8,128)(2,1)} %pad_maximum_fusion), channel_id=1, source_target_pairs={{0,1},{1,0},{2,3},{3,2},{4,5},{5,4},{6,7},{7,6},{8,9},{9,8},{10,11... | collective-permute-start | bytes 3538952 | tf_op jit(solution)/shard_map/ppermute | solution.py:440
  49.8 66.0 %collective-permute-start.11 = (bf16[2,384,768]{2,1,0:T(8,128)(2,1)}, bf16[2,384,768]{2,1,0:T(8,128)(2,1)}, u32[]{:S(2)}, u32[]{:S(2)}) collective-permute-start(bf16[2,384,768]{2,1,0:T(8,128)(2,1)} %pad_maximum_fusion.1), channel_id=1, source_target_pairs={{0,1},{1,0},{2,3},{3,2},{4,5},{5,4},{6,7},{7,6},{8,9},{9,8},{10,11... | collective-permute-start | bytes 3538952 | tf_op jit(solution)/shard_map/ppermute | solution.py:440
  57.5 16.8 %collective-permute-start.6 = (bf16[1,192,768]{2,1,0:T(8,128)(2,1)S(1)}, bf16[1,192,768]{2,1,0:T(8,128)(2,1)S(1)}, u32[]{:S(2)}, u32[]{:S(2)}) collective-permute-start(bf16[1,192,768]{2,1,0:T(8,128)(2,1)S(1)} %bitcast.102), channel_id=1, source_target_pairs={{0,2},{2,0},{4,6},{6,4},{8,10},{10,8},{12,14},{14,12},{16,18},{18,... | collective-permute-start | bytes 884744 | tf_op jit(solution)/shard_map/ppermute | solution.py:440
  57.6 32.7 %collective-permute-start.4 = (bf16[1,192,768]{2,1,0:T(8,128)(2,1)}, bf16[1,192,768]{2,1,0:T(8,128)(2,1)S(1)}, u32[]{:S(2)}, u32[]{:S(2)}) collective-permute-start(bf16[1,192,768]{2,1,0:T(8,128)(2,1)} %bitcast.15.near_ref), channel_id=1, source_target_pairs={{0,2},{2,0},{4,6},{6,4},{8,10},{10,8},{12,14},{14,12},{16,18},{18,... | collective-permute-start | bytes 884744 | tf_op jit(solution)/shard_map/ppermute | solution.py:440
  74.3 33.3 %copy-start.60 = (bf16[1024,256]{1,0:T(8,128)(2,1)}, bf16[1024,256]{1,0:T(8,128)(2,1)S(1)}, u32[]{:S(2)}) copy-start(bf16[1024,256]{1,0:T(8,128)(2,1)S(1)} %get-tuple-element.78.a0.att_ref) | copy-start | bytes 1572868
  74.3 33.3 %collective-permute-start.8 = (bf16[1,192,768]{2,1,0:T(8,128)(2,1)S(1)}, bf16[1,192,768]{2,1,0:T(8,128)(2,1)S(1)}, u32[]{:S(2)}, u32[]{:S(2)}) collective-permute-start(bf16[1,192,768]{2,1,0:T(8,128)(2,1)S(1)} %bitcast.100), channel_id=1, source_target_pairs={{0,2},{2,0},{4,6},{6,4},{8,10},{10,8},{12,14},{14,12},{16,18},{18,... | collective-permute-start | bytes 884744 | tf_op jit(solution)/shard_map/ppermute | solution.py:440
  90.4 17.3 %copy-start.62 = (bf16[1024,256]{1,0:T(8,128)(2,1)}, bf16[1024,256]{1,0:T(8,128)(2,1)S(1)}, u32[]{:S(2)}) copy-start(bf16[1024,256]{1,0:T(8,128)(2,1)S(1)} %get-tuple-element.82.a2.att_ref) | copy-start | bytes 1572868
  107.6 45.7 %collective-permute-start.10 = (bf16[1,2,384,768]{3,2,1,0:T(8,128)(2,1)}, bf16[1,2,384,768]{3,2,1,0:T(8,128)(2,1)}, u32[]{:S(2)}, u32[]{:S(2)}) collective-permute-start(bf16[1,2,384,768]{3,2,1,0:T(8,128)(2,1)} %bitcast.24), channel_id=1, source_target_pairs={{0,2},{2,0},{4,6},{6,4},{8,10},{10,8},{12,14},{14,12},{16,18},{18,... | collective-permute-start | bytes 3538952 | tf_op jit(solution)/shard_map/ppermute | solution.py:440
  115.8 18.0 %copy-start.59 = (bf16[1024,768]{1,0:T(8,128)(2,1)}, bf16[1024,768]{1,0:T(8,128)(2,1)S(1)}, u32[]{:S(2)}) copy-start(bf16[1024,768]{1,0:T(8,128)(2,1)S(1)} %get-tuple-element.85.n_ref) | copy-start | bytes 4718596
  115.8 59.0 %collective-permute-start.12 = (bf16[1,2,384,768]{3,2,1,0:T(8,128)(2,1)}, bf16[1,2,384,768]{3,2,1,0:T(8,128)(2,1)}, u32[]{:S(2)}, u32[]{:S(2)}) collective-permute-start(bf16[1,2,384,768]{3,2,1,0:T(8,128)(2,1)} %bitcast.29), channel_id=1, source_target_pairs={{0,2},{2,0},{4,6},{6,4},{8,10},{10,8},{12,14},{14,12},{16,18},{18,... | collective-permute-start | bytes 3538952 | tf_op jit(solution)/shard_map/ppermute | solution.py:440
  173.2 134.9 %collective-permute-start.33 = (bf16[768,768]{1,0:T(8,128)(2,1)}, bf16[768,768]{1,0:T(8,128)(2,1)}, u32[]{:S(2)}, u32[]{:S(2)}) collective-permute-start(bf16[768,768]{1,0:T(8,128)(2,1)} %get-tuple-element.138), channel_id=1, source_target_pairs={{0,2},{2,0},{4,6},{6,4},{8,10},{10,8},{12,14},{14,12},{16,18},{18,... | collective-permute-start | bytes 3538952 | tf_op jit(solution)/shard_map/ppermute | solution.py:440
  176.2 18.9 %copy-start.17 = (bf16[768,768]{1,0:T(8,128)(2,1)S(1)}, bf16[768,768]{1,0:T(8,128)(2,1)}, u32[]{:S(2)}) copy-start(bf16[768,768]{1,0:T(8,128)(2,1)} %copy-done.16) | copy-start | bytes 3538948
  176.2 18.9 %copy-start.26 = (bf16[256,1024]{1,0:T(8,128)(2,1)S(1)}, bf16[256,1024]{1,0:T(8,128)(2,1)}, u32[]{:S(2)}) copy-start(bf16[256,1024]{1,0:T(8,128)(2,1)} %copy-done.25) | copy-start | bytes 1572868
  176.2 18.9 %copy-start.28 = (bf16[256,1024]{1,0:T(8,128)(2,1)S(1)}, bf16[256,1024]{1,0:T(8,128)(2,1)}, u32[]{:S(2)}) copy-start(bf16[256,1024]{1,0:T(8,128)(2,1)} %copy-done.27) | copy-start | bytes 1572868
  176.2 18.9 %copy-start.30 = (bf16[256,1024]{1,0:T(8,128)(2,1)S(1)}, bf16[256,1024]{1,0:T(8,128)(2,1)}, u32[]{:S(2)}) copy-start(bf16[256,1024]{1,0:T(8,128)(2,1)} %copy-done.29) | copy-start | bytes 1572868
  237.4 72.7 %collective-permute-start.25 = (bf16[2,384,768]{2,1,0:T(8,128)(2,1)}, bf16[2,384,768]{2,1,0:T(8,128)(2,1)}, u32[]{:S(2)}, u32[]{:S(2)}) collective-permute-start(bf16[2,384,768]{2,1,0:T(8,128)(2,1)} %broadcast_select_fusion.4), channel_id=1, source_target_pairs={{0,2},{2,0},{4,6},{6,4},{8,10},{10,8},{12,14},{14,12},{16,18},{18,... | collective-permute-start | bytes 3538952 | tf_op jit(solution)/shard_map/ppermute | solution.py:440
  238.4 17.3 %copy-start.3 = (bf16[1024,768]{1,0:T(8,128)(2,1)S(1)}, bf16[1024,768]{1,0:T(8,128)(2,1)}, u32[]{:S(2)}) copy-start(bf16[1024,768]{1,0:T(8,128)(2,1)} %frames_ref.5) | copy-start | bytes 4718596
  238.4 17.3 %copy-start.70 = (bf16[768,768]{1,0:T(8,128)(2,1)S(1)}, bf16[768,768]{1,0:T(8,128)(2,1)}, u32[]{:S(2)}) copy-start(bf16[768,768]{1,0:T(8,128)(2,1)} %copy-done.69) | copy-start | bytes 3538948
  238.4 17.3 %copy-start.72 = (bf16[768,768]{1,0:T(8,128)(2,1)S(1)}, bf16[768,768]{1,0:T(8,128)(2,1)}, u32[]{:S(2)}) copy-start(bf16[768,768]{1,0:T(8,128)(2,1)} %copy-done.71) | copy-start | bytes 3538948
  238.4 17.3 %copy-start.74 = (bf16[768,768]{1,0:T(8,128)(2,1)S(1)}, bf16[768,768]{1,0:T(8,128)(2,1)}, u32[]{:S(2)}) copy-start(bf16[768,768]{1,0:T(8,128)(2,1)} %copy-done.73) | copy-start | bytes 3538948
  276.1 4.1 collective-permute-start.13
  281.0 1.2 collective-permute-start.14
  282.8 4.1 collective-permute-start.15
  284.6 81.1 %collective-permute-start.32 = (bf16[768,768]{1,0:T(8,128)(2,1)}, bf16[768,768]{1,0:T(8,128)(2,1)S(1)}, u32[]{:S(2)}, u32[]{:S(2)}) collective-permute-start(bf16[768,768]{1,0:T(8,128)(2,1)} %copy-done.54), channel_id=1, source_target_pairs={{0,2},{2,0},{4,6},{6,4},{8,10},{10,8},{12,14},{14,12},{16,18},{18,... | collective-permute-start | bytes 3538952 | tf_op jit(solution)/shard_map/ppermute | solution.py:440
  287.7 3.8 collective-permute-start.16
  291.2 22.4 %collective-permute-start.18 = (bf16[2,384,768]{2,1,0:T(8,128)(2,1)S(1)}, bf16[2,384,768]{2,1,0:T(8,128)(2,1)S(1)}, u32[]{:S(2)}, u32[]{:S(2)}) collective-permute-start(bf16[2,384,768]{2,1,0:T(8,128)(2,1)S(1)} %broadcast_select_fusion.5), channel_id=1, source_target_pairs={{0,2},{2,0},{4,6},{6,4},{8,10},{10,8},{12,14},{14,12},{16,18},{18,... | collective-permute-start | bytes 3538952 | tf_op jit(solution)/shard_map/ppermute | solution.py:440
  291.5 16.4 %collective-permute-start.17 = (f32[12,384]{1,0:T(8,128)S(1)}, f32[12,384]{1,0:T(8,128)S(1)}, u32[]{:S(2)}, u32[]{:S(2)}) collective-permute-start(f32[12,384]{1,0:T(8,128)S(1)} %add.176), channel_id=1, source_target_pairs={{0,16},{2,18},{4,20},{6,22},{8,24},{10,26},{12,28},{14,30},{16,0},... | collective-permute-start | bytes 55304 | tf_op jit(solution)/shard_map/ppermute | solution.py:440
  307.9 74.9 %collective-permute-start.40 = (bf16[768,768]{1,0:T(8,128)(2,1)S(1)}, bf16[768,768]{1,0:T(8,128)(2,1)S(1)}, u32[]{:S(2)}, u32[]{:S(2)}) collective-permute-start(bf16[768,768]{1,0:T(8,128)(2,1)S(1)} %copy-done.53), channel_id=1, source_target_pairs={{0,2},{2,0},{4,6},{6,4},{8,10},{10,8},{12,14},{14,12},{16,18},{18,... | collective-permute-start | bytes 3538952 | tf_op jit(solution)/shard_map/ppermute | solution.py:440
  308.1 7.2 %collective-permute-start.41 = (bf16[768,768]{1,0:T(8,128)(2,1)S(1)}, bf16[768,768]{1,0:T(8,128)(2,1)S(1)}, u32[]{:S(2)}, u32[]{:S(2)}) collective-permute-start(bf16[768,768]{1,0:T(8,128)(2,1)S(1)} %copy-done.56), channel_id=1, source_target_pairs={{0,2},{2,0},{4,6},{6,4},{8,10},{10,8},{12,14},{14,12},{16,18},{18,... | collective-permute-start | bytes 3538952 | tf_op jit(solution)/shard_map/ppermute | solution.py:440
  310.1 56.5 %collective-permute-start.34 = (bf16[768,768]{1,0:T(8,128)(2,1)S(1)}, bf16[768,768]{1,0:T(8,128)(2,1)S(1)}, u32[]{:S(2)}, u32[]{:S(2)}) collective-permute-start(bf16[768,768]{1,0:T(8,128)(2,1)S(1)} %add_convert_fusion.4), channel_id=1, source_target_pairs={{0,1},{1,0},{2,3},{3,2},{4,5},{5,4},{6,7},{7,6},{8,9},{9,8},{10,11... | collective-permute-start | bytes 3538952 | tf_op jit(solution)/shard_map/ppermute | solution.py:440
  313.6 38.0 %collective-permute-start.26 = (bf16[384,768]{1,0:T(8,128)(2,1)S(1)}, bf16[384,768]{1,0:T(8,128)(2,1)S(1)}, u32[]{:S(2)}, u32[]{:S(2)}) collective-permute-start(bf16[384,768]{1,0:T(8,128)(2,1)S(1)} %slice_bitcast_fusion), channel_id=1, source_target_pairs={{0,1},{1,0},{2,3},{3,2},{4,5},{5,4},{6,7},{7,6},{8,9},{9,8},{10,11... | collective-permute-start | bytes 1769480 | tf_op jit(solution)/shard_map/ppermute | solution.py:440
  315.3 49.0 %collective-permute-start.19 = (bf16[384,768]{1,0:T(8,128)(2,1)S(1)}, bf16[384,768]{1,0:T(8,128)(2,1)S(1)}, u32[]{:S(2)}, u32[]{:S(2)}) collective-permute-start(bf16[384,768]{1,0:T(8,128)(2,1)S(1)} %slice_bitcast_fusion.2), channel_id=1, source_target_pairs={{0,1},{1,0},{2,3},{3,2},{4,5},{5,4},{6,7},{7,6},{8,9},{9,8},{10,11... | collective-permute-start | bytes 1769480 | tf_op jit(solution)/shard_map/ppermute | solution.py:440
  351.6 37.2 %collective-permute-start.42 = (bf16[768,768]{1,0:T(8,128)(2,1)S(1)}, bf16[768,768]{1,0:T(8,128)(2,1)S(1)}, u32[]{:S(2)}, u32[]{:S(2)}) collective-permute-start(bf16[768,768]{1,0:T(8,128)(2,1)S(1)} %add_convert_fusion.1), channel_id=1, source_target_pairs={{0,1},{1,0},{2,3},{3,2},{4,5},{5,4},{6,7},{7,6},{8,9},{9,8},{10,11... | collective-permute-start | bytes 3538952 | tf_op jit(solution)/shard_map/ppermute | solution.py:440
  364.3 9.9 %collective-permute-start.27 = (bf16[192,768]{1,0:T(8,128)(2,1)S(1)}, bf16[192,768]{1,0:T(8,128)(2,1)S(1)}, u32[]{:S(2)}, u32[]{:S(2)}) collective-permute-start(bf16[192,768]{1,0:T(8,128)(2,1)S(1)} %constant_dynamic-slice_fusion.2), channel_id=1, source_target_pairs={{0,4},{2,6},{4,0},{6,2},{8,12},{10,14},{12,8},{14,10},{16,20},{18,... | collective-permute-start | bytes 884744 | tf_op jit(solution)/shard_map/ppermute | solution.py:440
  365.7 14.9 %collective-permute-start.20 = (bf16[192,768]{1,0:T(8,128)(2,1)S(1)}, bf16[192,768]{1,0:T(8,128)(2,1)S(1)}, u32[]{:S(2)}, u32[]{:S(2)}) collective-permute-start(bf16[192,768]{1,0:T(8,128)(2,1)S(1)} %constant_dynamic-slice_fusion.3), channel_id=1, source_target_pairs={{0,4},{2,6},{4,0},{6,2},{8,12},{10,14},{12,8},{14,10},{16,20},{18,... | collective-permute-start | bytes 884744 | tf_op jit(solution)/shard_map/ppermute | solution.py:440
  367.1 21.7 %copy-start.13 = (bf16[768,768]{1,0:T(8,128)(2,1)S(1)}, bf16[768,768]{1,0:T(8,128)(2,1)}, u32[]{:S(2)}) copy-start(bf16[768,768]{1,0:T(8,128)(2,1)} %copy-done.12) | copy-start | bytes 3538948
  367.1 26.5 %collective-permute-start.35 = (bf16[384,768]{1,0:T(8,128)(2,1)S(1)}, bf16[384,768]{1,0:T(8,128)(2,1)S(1)}, u32[]{:S(2)}, u32[]{:S(2)}) collective-permute-start(bf16[384,768]{1,0:T(8,128)(2,1)S(1)} %constant_dynamic-slice_fusion.1), channel_id=1, source_target_pairs={{0,4},{2,6},{4,0},{6,2},{8,12},{10,14},{12,8},{14,10},{16,20},{18,... | collective-permute-start | bytes 1769480 | tf_op jit(solution)/shard_map/ppermute | solution.py:440
  374.3 16.1 %collective-permute-start.28 = (bf16[192,768]{1,0:T(8,128)(2,1)S(1)}, bf16[192,768]{1,0:T(8,128)(2,1)S(1)}, u32[]{:S(2)}, u32[]{:S(2)}) collective-permute-start(bf16[192,768]{1,0:T(8,128)(2,1)S(1)} %add_convert_fusion.16), channel_id=1, source_target_pairs={{0,8},{2,10},{4,12},{6,14},{8,0},{10,2},{12,4},{14,6},{16,24},{18,... | collective-permute-start | bytes 884744 | tf_op jit(solution)/shard_map/ppermute | solution.py:440
  380.6 11.1 %collective-permute-start.21 = (bf16[192,768]{1,0:T(8,128)(2,1)S(1)}, bf16[192,768]{1,0:T(8,128)(2,1)S(1)}, u32[]{:S(2)}, u32[]{:S(2)}) collective-permute-start(bf16[192,768]{1,0:T(8,128)(2,1)S(1)} %add_convert_fusion.19), channel_id=1, source_target_pairs={{0,8},{2,10},{4,12},{6,14},{8,0},{10,2},{12,4},{14,6},{16,24},{18,... | collective-permute-start | bytes 884744 | tf_op jit(solution)/shard_map/ppermute | solution.py:440
  389.4 30.3 %collective-permute-start.43 = (bf16[384,768]{1,0:T(8,128)(2,1)S(1)}, bf16[384,768]{1,0:T(8,128)(2,1)S(1)}, u32[]{:S(2)}, u32[]{:S(2)}) collective-permute-start(bf16[384,768]{1,0:T(8,128)(2,1)S(1)} %constant_dynamic-slice_fusion), channel_id=1, source_target_pairs={{0,4},{2,6},{4,0},{6,2},{8,12},{10,14},{12,8},{14,10},{16,20},{18,... | collective-permute-start | bytes 1769480 | tf_op jit(solution)/shard_map/ppermute | solution.py:440
  390.5 22.9 %collective-permute-start.29 = (bf16[192,768]{1,0:T(8,128)(2,1)S(1)}, bf16[192,768]{1,0:T(8,128)(2,1)S(1)}, u32[]{:S(2)}, u32[]{:S(2)}) collective-permute-start(bf16[192,768]{1,0:T(8,128)(2,1)S(1)} %add_convert_fusion.15), channel_id=1, source_target_pairs={{0,16},{2,18},{4,20},{6,22},{8,24},{10,26},{12,28},{14,30},{16,0},... | collective-permute-start | bytes 884744 | tf_op jit(solution)/shard_map/ppermute | solution.py:440
  391.8 26.6 %collective-permute-start.22 = (bf16[192,768]{1,0:T(8,128)(2,1)S(1)}, bf16[192,768]{1,0:T(8,128)(2,1)S(1)}, u32[]{:S(2)}, u32[]{:S(2)}) collective-permute-start(bf16[192,768]{1,0:T(8,128)(2,1)S(1)} %add_convert_fusion.18), channel_id=1, source_target_pairs={{0,16},{2,18},{4,20},{6,22},{8,24},{10,26},{12,28},{14,30},{16,0},... | collective-permute-start | bytes 884744 | tf_op jit(solution)/shard_map/ppermute | solution.py:440
  393.8 33.8 %collective-permute-start.36 = (bf16[384,768]{1,0:T(8,128)(2,1)S(1)}, bf16[384,768]{1,0:T(8,128)(2,1)}, u32[]{:S(2)}, u32[]{:S(2)}) collective-permute-start(bf16[384,768]{1,0:T(8,128)(2,1)S(1)} %add_convert_fusion.13), channel_id=1, source_target_pairs={{0,8},{2,10},{4,12},{6,14},{8,0},{10,2},{12,4},{14,6},{16,24},{18,... | collective-permute-start | bytes 1769480 | tf_op jit(solution)/shard_map/ppermute | solution.py:440
  413.5 13.4 %collective-permute-start.30 = (bf16[192,768]{1,0:T(8,128)(2,1)S(1)}, bf16[192,768]{1,0:T(8,128)(2,1)S(1)}, u32[]{:S(2)}, u32[]{:S(2)}) collective-permute-start(bf16[192,768]{1,0:T(8,128)(2,1)S(1)} %add_convert_fusion.14), channel_id=1, source_target_pairs={{0,4},{2,6},{4,0},{6,2},{8,12},{10,14},{12,8},{14,10},{16,20},{18,... | collective-permute-start | bytes 884744 | tf_op jit(solution)/shard_map/ppermute | solution.py:440
  418.4 8.2 %collective-permute-start.23 = (bf16[192,768]{1,0:T(8,128)(2,1)S(1)}, bf16[192,768]{1,0:T(8,128)(2,1)S(1)}, u32[]{:S(2)}, u32[]{:S(2)}) collective-permute-start(bf16[192,768]{1,0:T(8,128)(2,1)S(1)} %add_convert_fusion.17), channel_id=1, source_target_pairs={{0,4},{2,6},{4,0},{6,2},{8,12},{10,14},{12,8},{14,10},{16,20},{18,... | collective-permute-start | bytes 884744 | tf_op jit(solution)/shard_map/ppermute | solution.py:440
  419.8 15.8 %collective-permute-start.44 = (bf16[384,768]{1,0:T(8,128)(2,1)S(1)}, bf16[384,768]{1,0:T(8,128)(2,1)}, u32[]{:S(2)}, u32[]{:S(2)}) collective-permute-start(bf16[384,768]{1,0:T(8,128)(2,1)S(1)} %add_convert_fusion.10), channel_id=1, source_target_pairs={{0,8},{2,10},{4,12},{6,14},{8,0},{10,2},{12,4},{14,6},{16,24},{18,... | collective-permute-start | bytes 1769480 | tf_op jit(solution)/shard_map/ppermute | solution.py:440
  426.8 10.5 %collective-permute-start.24 = (bf16[384,768]{1,0:T(8,128)(2,1)S(1)}, bf16[384,768]{1,0:T(8,128)(2,1)S(1)}, u32[]{:S(2)}, u32[]{:S(2)}) collective-permute-start(bf16[384,768]{1,0:T(8,128)(2,1)S(1)} %maximum_select_fusion.2), channel_id=1, source_target_pairs={{0,2},{2,0},{4,6},{6,4},{8,10},{10,8},{12,14},{14,12},{16,18},{18,... | collective-permute-start | bytes 1769480 | tf_op jit(solution)/shard_map/ppermute | solution.py:440
  427.1 11.4 %collective-permute-start.31 = (bf16[384,768]{1,0:T(8,128)(2,1)S(1)}, bf16[384,768]{1,0:T(8,128)(2,1)S(1)}, u32[]{:S(2)}, u32[]{:S(2)}) collective-permute-start(bf16[384,768]{1,0:T(8,128)(2,1)S(1)} %maximum_select_fusion.3), channel_id=1, source_target_pairs={{0,2},{2,0},{4,6},{6,4},{8,10},{10,8},{12,14},{14,12},{16,18},{18,... | collective-permute-start | bytes 1769480 | tf_op jit(solution)/shard_map/ppermute | solution.py:440
  428.8 42.4 %collective-permute-start.37 = (bf16[384,768]{1,0:T(8,128)(2,1)S(1)}, bf16[384,768]{1,0:T(8,128)(2,1)S(1)}, u32[]{:S(2)}, u32[]{:S(2)}) collective-permute-start(bf16[384,768]{1,0:T(8,128)(2,1)S(1)} %add_convert_fusion.12), channel_id=1, source_target_pairs={{0,16},{2,18},{4,20},{6,22},{8,24},{10,26},{12,28},{14,30},{16,0},... | collective-permute-start | bytes 1769480 | tf_op jit(solution)/shard_map/ppermute | solution.py:440
  436.9 46.1 %collective-permute-start.45 = (bf16[384,768]{1,0:T(8,128)(2,1)S(1)}, bf16[384,768]{1,0:T(8,128)(2,1)S(1)}, u32[]{:S(2)}, u32[]{:S(2)}) collective-permute-start(bf16[384,768]{1,0:T(8,128)(2,1)S(1)} %add_convert_fusion.9), channel_id=1, source_target_pairs={{0,16},{2,18},{4,20},{6,22},{8,24},{10,26},{12,28},{14,30},{16,0},... | collective-permute-start | bytes 1769480 | tf_op jit(solution)/shard_map/ppermute | solution.py:440
  471.4 13.6 %collective-permute-start.38 = (bf16[384,768]{1,0:T(8,128)(2,1)S(1)}, bf16[384,768]{1,0:T(8,128)(2,1)S(1)}, u32[]{:S(2)}, u32[]{:S(2)}) collective-permute-start(bf16[384,768]{1,0:T(8,128)(2,1)S(1)} %add_convert_fusion.11), channel_id=1, source_target_pairs={{0,4},{2,6},{4,0},{6,2},{8,12},{10,14},{12,8},{14,10},{16,20},{18,... | collective-permute-start | bytes 1769480 | tf_op jit(solution)/shard_map/ppermute | solution.py:440
  483.1 14.5 %collective-permute-start.46 = (bf16[384,768]{1,0:T(8,128)(2,1)S(1)}, bf16[384,768]{1,0:T(8,128)(2,1)S(1)}, u32[]{:S(2)}, u32[]{:S(2)}) collective-permute-start(bf16[384,768]{1,0:T(8,128)(2,1)S(1)} %add_convert_fusion.8), channel_id=1, source_target_pairs={{0,4},{2,6},{4,0},{6,2},{8,12},{10,14},{12,8},{14,10},{16,20},{18,... | collective-permute-start | bytes 1769480 | tf_op jit(solution)/shard_map/ppermute | solution.py:440
  485.4 14.8 %collective-permute-start.39 = (bf16[768,768]{1,0:T(8,128)(2,1)S(1)}, bf16[768,768]{1,0:T(8,128)(2,1)S(1)}, u32[]{:S(2)}, u32[]{:S(2)}) collective-permute-start(bf16[768,768]{1,0:T(8,128)(2,1)S(1)} %maximum_select_fusion), channel_id=1, source_target_pairs={{0,2},{2,0},{4,6},{6,4},{8,10},{10,8},{12,14},{14,12},{16,18},{18,... | collective-permute-start | bytes 3538952 | tf_op jit(solution)/shard_map/ppermute | solution.py:440
  498.1 2.9 collective-permute-start.47
  (81 other events, 376.0 us)
